TPU v7x, 32 devices: a whole 2x2x4 slice. The times are simulated.
32 devices in a mesh: blk: 16 (over z, x, core), mp: 2 (over y).
Axes of the slice: x: 2, y: 2, z: 4, core: 2. Of those that a mesh axis runs over, the one named last changes fastest.
Arguments:
- anchors: bfloat16 [8192, 1024], P('blk', 'mp'), may hold values from -0.5833631 to 0.5833631, as said below
- partners: bfloat16 [8192, 1024], P('blk', 'mp'), may hold values from -0.5833631 to 0.5833631, as said below
- row_lse: float32 [8192], P('blk'), as said below
- anchor_acc: float32 [8192, 1024], P('blk', 'mp'), may hold values from -6 to 6
- partner_acc: float32 [8192, 1024], P('blk', 'mp'), may hold values from -6 to 6
- match_dev: int32 [8192], P('blk'), may hold values from 0 to 15, as said below
- match_row: int32 [8192], P('blk'), may hold values from 0 to 511
Outputs:
- anchor_grad: float32 [8192, 1024], P('blk', 'mp')
- partner_out: float32 [8192, 1024], P('blk', 'mp')
Inputs may be any that keep to these rules, and one draw needn't show every extreme that they name: Within each block of 512 rows every block index appears exactly 32 times, and the pairs (match_dev, match_row) name every partner row exactly once. `anchors`: entries are independent with mean 0 and standard deviation 0.55 / 1024 ** 0.25. `partners`: entries are independent with mean 0 and standard deviation 0.55 / 1024 ** 0.25. `row_lse`: each entry lies within 1.5 of log(1024) + 4.5.
All inputs are finite; a program needn't handle non-finite values.
Results may differ from a plain program's by a relative error of at most 0.0085.
Values may be sent and summed in bfloat16 or wider, within the bound.
No kernel may reach another device: no remote copies, remote signals or barrier semaphores. Data moves between devices by JAX's collectives and lax.ppermute only.
A program may use at most 64 MiB of HBM per device.

v0:
```python
import jax
import jax.numpy as jnp
from jax import lax
from jax.sharding import PartitionSpec as P

SCALE = 10.0


def shifted(value, axis, steps):
    count = lax.axis_size(axis)
    pairs = [(source, (source + steps) % count) for source in range(count)]
    return lax.ppermute(value, axis, pairs)


def contract_rows(left, right):
    return lax.dot_general(
        left, right, (((1,), (1,)), ((), ())), preferred_element_type=jnp.float32
    )


def contract_cols(left, right):
    return lax.dot_general(
        left, right, (((0,), (0,)), ((), ())), preferred_element_type=jnp.float32
    )


def on_device(anchors, partners, row_lse, anchor_acc, partner_acc, match_dev, match_row):
    row_count = anchors.shape[0]
    width = anchors.shape[1]
    blocks = lax.axis_size("blk")
    per_peer = row_count // blocks
    previous = shifted(partners, "blk", 1)
    ordering = jnp.argsort(match_dev, stable=True)
    wanted = jnp.take(match_row, ordering).reshape(blocks, per_peer)
    requested = lax.all_to_all(wanted, "blk", split_axis=0, concat_axis=0, tiled=True)
    requested_flat = requested.reshape(-1)
    found_rows = jnp.take(partners, requested_flat, axis=0).reshape(blocks, per_peer, width)
    sorted_anchors = jnp.take(anchors, ordering, axis=0).reshape(blocks, per_peer, width)
    fetched = lax.all_to_all(found_rows, "blk", split_axis=0, concat_axis=0, tiled=True)
    grad_slots = -SCALE * sorted_anchors.astype(jnp.float32)
    returned = lax.all_to_all(
        grad_slots.astype(jnp.bfloat16), "blk", split_axis=0, concat_axis=0, tiled=True
    ).astype(grad_slots.dtype)
    home = (
        jnp.zeros((row_count, width), jnp.float32)
        .at[requested_flat]
        .set(returned.reshape(row_count, width))
    )
    positive = jnp.zeros_like(partners).at[ordering].set(fetched.reshape(row_count, width))
    lse_column = row_lse[:, None]
    partial_own = contract_rows(anchors, partners)
    partial_prior = contract_rows(anchors, previous)
    summed_own, summed_prior = lax.psum((partial_own, partial_prior), "mp")
    weight_own = jnp.exp(SCALE * summed_own - lse_column).astype(jnp.bfloat16)
    weight_prior = jnp.exp(SCALE * summed_prior - lse_column).astype(jnp.bfloat16)
    toward = SCALE * (
        jnp.dot(weight_own, partners, preferred_element_type=jnp.float32)
        + jnp.dot(weight_prior, previous, preferred_element_type=jnp.float32)
    )
    anchor_grad = anchor_acc + toward - SCALE * positive.astype(jnp.float32)
    own_terms = SCALE * contract_cols(weight_own, anchors)
    staying = partner_acc + home + own_terms
    arrived = shifted(staying, "blk", 1)
    partner_out = arrived + SCALE * contract_cols(weight_prior, anchors)
    return (anchor_grad, partner_out)


def solution(mesh):
    return jax.shard_map(
        on_device,
        mesh=mesh,
        in_specs=(
            P("blk", "mp"),
            P("blk", "mp"),
            P("blk"),
            P("blk", "mp"),
            P("blk", "mp"),
            P("blk"),
            P("blk"),
        ),
        out_specs=(P("blk", "mp"), P("blk", "mp")),
        check_vma=False,
    )
```

profile of v0, /device:TPU:0, one launch (start us, length us, event | category | flops | bytes accessed | tf_op | source)
XLA Modules:
  0.0 114.5 jit_solution(17748089162269643928)
XLA Ops:
  7.2 0.0 copy-start
  7.2 0.0 all-reduce.3.cloned.1.call-start
  7.2 0.5 collective-permute-start
  7.7 0.5 copy-done
  8.2 2.5 %fusion.11 = f32[512,512]{1,0:T(8,128)} fusion(bf16[512,512]{1,0:T(8,128)(2,1)S(1)} %copy-done, bf16[512,512]{1,0:T(8,128)(2,1)} %param.10), kind=kOutput, calls=%fused_computation.31 | convolution fusion | flops 268435456 | bytes 2097152 | tf_op jit(solution)/shard_map/dot_general | solution.py:16
  10.7 9.1 %collective-permute-done = bf16[512,512]{1,0:T(8,128)(2,1)S(1)} collective-permute-done((bf16[512,512]{1,0:T(8,128)(2,1)}, bf16[512,512]{1,0:T(8,128)(2,1)S(1)}, u32[]{:S(2)}, u32[]{:S(2)}) %collective-permute-start) | collective-permute-done | bytes 524320 | tf_op jit(solution)/shard_map/ppermute | solution.py:12
  19.8 0.0 copy-start.5
  19.8 0.8 copy-done.5
  20.6 1.4 %fusion.12 = f32[512,512]{1,0:T(8,128)} fusion(bf16[512,512]{1,0:T(8,128)(2,1)S(1)} %copy-done, bf16[512,512]{1,0:T(8,128)(2,1)S(1)} %collective-permute-done), kind=kOutput, calls=%fused_computation.32 | convolution fusion | flops 268435456 | bytes 2097152 | tf_op jit(solution)/shard_map/dot_general | solution.py:16
  22.0 0.0 all-reduce.3.cloned.1.call-update
  22.0 0.0 copy-start.9
  22.1 0.7 copy-done.9
  22.7 3.8 %sort.17 = (s32[512]{0:T(512)}, s32[512]{0:T(512)S(1)}) sort(s32[512]{0:T(512)S(1)} %copy-done.9, s32[512]{0:T(512)S(1)} %iota.4), dimensions={0}, to_apply=%region_2.3 | sort | flops 4608 | bytes 8192 | tf_op jit(solution)/shard_map/jit(argsort)/sort | solution.py:33
  26.5 0.7 copy-done.1
  27.2 3.5 %gather_fusion = s32[512]{0:T(512)S(1)} fusion(s32[512]{0:T(512)S(1)} %copy-done.1, s32[1024]{0:T(1024)S(1)} %pad_clamp_fusion.1), kind=kCustom, calls=%fused_computation.2 | custom fusion | bytes 6144 | tf_op jit(solution)/shard_map/jit(_take)/gather | solution.py:34
  30.7 0.7 select_n.39
  31.4 3.7 %all-to-all-start = ((s32[16,1,32]{2,1,0:T(1,128)}), s32[16,1,32]{2,1,0:T(1,128)S(1)}, u32[]{:S(2)}, u32[]{:S(2)}) async-start(s32[16,1,32]{2,1,0:T(1,128)} %select_n.39), calls=%async_computation | async-start | bytes 16384 | tf_op jit(solution)/shard_map/all_to_all | solution.py:35
  35.0 2.0 %gather_fusion.2 = bf16[512,512]{1,0:T(8,128)(2,1)S(1)} fusion(bf16[512,512]{1,0:T(8,128)(2,1)S(1)} %copy-done, s32[1024]{0:T(1024)S(1)} %pad_clamp_fusion.1), kind=kCustom, calls=%fused_computation.1.clone | custom fusion | bytes 1050624 | tf_op jit(solution)/shard_map/jit(_take)/gather | solution.py:38
  37.0 1.0 multiply_convert_fusion
  38.0 3.4 %all-to-all-done = s32[16,1,32]{2,1,0:T(1,128)S(1)} async-done(((s32[16,1,32]{2,1,0:T(1,128)}), s32[16,1,32]{2,1,0:T(1,128)S(1)}, u32[]{:S(2)}, u32[]{:S(2)}) %all-to-all-start) | async-done | bytes 2080 | tf_op jit(solution)/shard_map/all_to_all | solution.py:35
  41.5 3.7 %all-to-all-start.2 = ((bf16[16,32,512]{2,1,0:T(8,128)(2,1)}), bf16[16,32,512]{2,1,0:T(8,128)(2,1)S(1)}, u32[]{:S(2)}, u32[]{:S(2)}) async-start(bf16[16,32,512]{2,1,0:T(8,128)(2,1)} %bitcast.3), calls=%async_computation.2 | async-start | bytes 1048576 | tf_op jit(solution)/shard_map/all_to_all | solution.py:41
  45.2 0.6 broadcast.90
  45.8 0.7 reduce.5
  46.5 0.1 reshape.91
  46.6 0.0 copy-done.2
  46.6 2.0 %gather_fusion.1 = bf16[512,512]{1,0:T(8,128)(2,1)S(1)} fusion(bf16[512,512]{1,0:T(8,128)(2,1)S(1)} %copy-done.2, s32[1024]{0:T(1024)S(1)} %pad_clamp_fusion), kind=kCustom, calls=%fused_computation.clone | custom fusion | bytes 1050624 | tf_op jit(solution)/shard_map/jit(_take)/gather | solution.py:37
  48.6 0.9 broadcast_select_fusion
  49.5 10.1 %all-to-all-done.2 = bf16[16,32,512]{2,1,0:T(8,128)(2,1)S(1)} async-done(((bf16[16,32,512]{2,1,0:T(8,128)(2,1)}), bf16[16,32,512]{2,1,0:T(8,128)(2,1)S(1)}, u32[]{:S(2)}, u32[]{:S(2)}) %all-to-all-start.2) | async-done | bytes 524320 | tf_op jit(solution)/shard_map/all_to_all | solution.py:41
  59.6 4.2 %all-to-all-start.1 = ((bf16[16,32,512]{2,1,0:T(8,128)(2,1)}), bf16[16,32,512]{2,1,0:T(8,128)(2,1)}, u32[]{:S(2)}, u32[]{:S(2)}) async-start(bf16[16,32,512]{2,1,0:T(8,128)(2,1)} %bitcast), calls=%async_computation.1 | async-start | bytes 1048576 | tf_op jit(solution)/shard_map/all_to_all | solution.py:39
  63.8 0.1 reshape.94
  63.9 2.6 %scatter_custom_fusion.1 = f32[512,512]{1,0:T(8,128)S(1)} fusion(s32[512]{0:T(512)S(1)} %bitcast.17, bf16[512,512]{1,0:T(8,128)(2,1)S(1)} %bitcast.15, f32[]{:T(128)} %constant.22.clone.1), kind=kCustom, calls=%fused_computation.13 | custom fusion | flops 262144 | bytes 1572868 | tf_op jit(solution)/shard_map/scatter | solution.py:47
  66.5 17.9 %all-reduce.3.cloned.1.call-done = (f32[512,512]{1,0:T(8,128)}, f32[512,512]{1,0:T(8,128)}) async-done(((f32[512,512]{1,0:T(8,128)}, f32[512,512]{1,0:T(8,128)}), (f32[512,512]{1,0:T(8,128)}, f32[512,512]{1,0:T(8,128)})) %all-reduce.3.cloned.1.call-update) | async-done | bytes 2097168 | tf_op jit(solution)/shard_map/psum | solution.py:53
  84.4 0.0 copy-done.8
  84.4 3.2 %fusion.1 = f32[512,512]{1,0:T(8,128)} fusion(bf16[512,512]{1,0:T(8,128)(2,1)S(1)} %copy-done, f32[512,512]{1,0:T(8,128)} %param.13, f32[512,512]{1,0:T(8,128)S(1)} %scatter_custom_fusion.1, f32[512,512]{1,0:T(8,128)} %get-tuple-element.5, f32[512]{0:T(512)S(1)} %copy-done.8), kind=kOutput, calls=%fused_computation.8 | convolution fusion | flops 270008320 | bytes 4720640 | tf_op jit(solution)/shard_map/dot_general | solution.py:22
  87.6 0.0 collective-permute-start.1
  87.6 0.0 all-to-all-done.1
  87.6 3.0 %scatter_custom_fusion = bf16[512,512]{1,0:T(8,128)(2,1)S(1)} fusion(s32[512]{0:T(512)S(1)} %compare_select_fusion.2, bf16[512,512]{1,0:T(8,128)(2,1)} %bitcast.1, bf16[]{:T(256)} %constant.9.clone.1), kind=kCustom, calls=%fused_computation.20 | custom fusion | bytes 524800 | tf_op jit(solution)/shard_map/scatter | solution.py:49
  90.6 0.0 copy-done.4
  90.7 0.0 copy-start.3
  90.7 0.0 copy-start.6
  90.7 0.0 copy-start.7
  90.7 0.5 fusion.10
  91.2 0.7 copy-done.3
  91.9 0.1 copy-done.6
  92.0 0.3 copy-done.7
  92.4 1.5 %fusion.4 = f32[512,512]{1,0:T(8,128)} fusion(f32[512,512]{1,0:T(8,128)S(1)} %copy-done.7, f32[512,512]{1,0:T(8,128)S(1)} %fusion.10, bf16[512,512]{1,0:T(8,128)(2,1)S(1)} %copy-done.6, bf16[512,512]{1,0:T(8,128)(2,1)S(1)} %scatter_custom_fusion, f32[512,512]{1,0:T(8,128)S(1)} %copy-done.3, f32[512]{0:T(512)S(1)} %copy-done.8), kind=kOutput, calls=%fused_computation.12 | convolution fusion | flops 270794752 | bytes 5244928 | tf_op jit(solution)/shard_map/dot_general | solution.py:58
  93.9 11.0 %collective-permute-done.1 = f32[512,512]{1,0:T(8,128)} collective-permute-done((f32[512,512]{1,0:T(8,128)}, f32[512,512]{1,0:T(8,128)}, u32[]{:S(2)}, u32[]{:S(2)}) %collective-permute-start.1) | collective-permute-done | bytes 1048608 | tf_op jit(solution)/shard_map/ppermute | solution.py:12
  104.9 2.8 %fusion = f32[512,512]{1,0:T(8,128)} fusion(f32[512,512]{1,0:T(8,128)} %collective-permute-done.1, bf16[512,512]{1,0:T(8,128)(2,1)S(1)} %copy-done, f32[512,512]{1,0:T(8,128)S(1)} %copy-done.3, f32[512]{0:T(512)S(1)} %copy-done.8), kind=kOutput, calls=%fused_computation.6 | convolution fusion | flops 269746176 | bytes 3672064 | tf_op jit(solution)/shard_map/dot_general | solution.py:22
  (12 shorter events, 0.1 us)
Async XLA Ops:
  7.2 1.0 copy-start
  7.2 77.2 %all-reduce.3.cloned.1.call-start = ((), (), s32[]{:S(2)}) async-start(), calls=%async_computation.3 | async-start | bytes 4194304 | tf_op jit(solution)/shard_map/psum | solution.py:53
  7.2 12.5 %collective-permute-start = (bf16[512,512]{1,0:T(8,128)(2,1)}, bf16[512,512]{1,0:T(8,128)(2,1)S(1)}, u32[]{:S(2)}, u32[]{:S(2)}) collective-permute-start(bf16[512,512]{1,0:T(8,128)(2,1)} %param.10), channel_id=1, source_target_pairs={{0,2},{2,4},{4,6},{6,8},{8,10},{10,12},{12,14},{14,16},{16,18},{18... | collective-permute-start | bytes 1572872 | tf_op jit(solution)/shard_map/ppermute | solution.py:12
  19.8 0.8 copy-start.5
  22.0 0.7 copy-start.9
  26.5 0.7 copy-start.1
  31.4 10.1 %all-to-all-start = ((s32[16,1,32]{2,1,0:T(1,128)}), s32[16,1,32]{2,1,0:T(1,128)S(1)}, u32[]{:S(2)}, u32[]{:S(2)}) async-start(s32[16,1,32]{2,1,0:T(1,128)} %select_n.39), calls=%async_computation | async-start | bytes 16384 | tf_op jit(solution)/shard_map/all_to_all | solution.py:35
  41.4 5.1 %copy-start.2 = (bf16[512,512]{1,0:T(8,128)(2,1)S(1)}, bf16[512,512]{1,0:T(8,128)(2,1)}, u32[]{:S(2)}) copy-start(bf16[512,512]{1,0:T(8,128)(2,1)} %param.10) | copy-start | bytes 1572868
  41.5 18.1 %all-to-all-start.2 = ((bf16[16,32,512]{2,1,0:T(8,128)(2,1)}), bf16[16,32,512]{2,1,0:T(8,128)(2,1)S(1)}, u32[]{:S(2)}, u32[]{:S(2)}) async-start(bf16[16,32,512]{2,1,0:T(8,128)(2,1)} %bitcast.3), calls=%async_computation.2 | async-start | bytes 1048576 | tf_op jit(solution)/shard_map/all_to_all | solution.py:41
  59.6 28.0 %all-to-all-start.1 = ((bf16[16,32,512]{2,1,0:T(8,128)(2,1)}), bf16[16,32,512]{2,1,0:T(8,128)(2,1)}, u32[]{:S(2)}, u32[]{:S(2)}) async-start(bf16[16,32,512]{2,1,0:T(8,128)(2,1)} %bitcast), calls=%async_computation.1 | async-start | bytes 1048576 | tf_op jit(solution)/shard_map/all_to_all | solution.py:39
  63.9 20.4 %copy-start.8 = (f32[512]{0:T(512)S(1)}, f32[512]{0:T(512)}, u32[]{:S(2)}) copy-start(f32[512]{0:T(512)} %param.11) | copy-start | bytes 6148
  84.4 6.3 %copy-start.4 = (f32[512,512]{1,0:T(8,128)S(1)}, f32[512,512]{1,0:T(8,128)}, u32[]{:S(2)}) copy-start(f32[512,512]{1,0:T(8,128)} %get-tuple-element.5) | copy-start | bytes 3145732
  87.6 17.2 %collective-permute-start.1 = (f32[512,512]{1,0:T(8,128)}, f32[512,512]{1,0:T(8,128)}, u32[]{:S(2)}, u32[]{:S(2)}) collective-permute-start(f32[512,512]{1,0:T(8,128)} %fusion.1), channel_id=1, source_target_pairs={{0,2},{2,4},{4,6},{6,8},{8,10},{10,12},{12,14},{14,16},{16,18},{18... | collective-permute-start | bytes 3145736 | tf_op jit(solution)/shard_map/ppermute | solution.py:12
  90.7 1.2 %copy-start.3 = (f32[512,512]{1,0:T(8,128)S(1)}, f32[512,512]{1,0:T(8,128)}, u32[]{:S(2)}) copy-start(f32[512,512]{1,0:T(8,128)} %get-tuple-element.6) | copy-start | bytes 3145732
  90.7 1.3 %copy-start.6 = (bf16[512,512]{1,0:T(8,128)(2,1)S(1)}, bf16[512,512]{1,0:T(8,128)(2,1)}, u32[]{:S(2)}) copy-start(bf16[512,512]{1,0:T(8,128)(2,1)} %copy-done.5) | copy-start | bytes 1572868
  90.7 1.7 %copy-start.7 = (f32[512,512]{1,0:T(8,128)S(1)}, f32[512,512]{1,0:T(8,128)}, u32[]{:S(2)}) copy-start(f32[512,512]{1,0:T(8,128)} %param.12) | copy-start | bytes 3145732
Sparse Core Ops, SparseCore 0:
  22.1 62.1 all-reduce.2
where the time goes:
time: 115 us
  waiting for transfers between devices  51.5 us (45%)
  local copies, waits for them, and re-layouts  15.7 us (14%)
  between operations  14.2 us (12%)
  starting transfers between devices  12.2 us (11%)
  matrix products  12 us (10%)
  other arithmetic  9.04 us (8%)
    ppermute x2, waiting for transfers between devices, shifted(): return lax.ppermute(value, axis, pairs)  20.1 us
    psum x1, waiting for transfers between devices, on_device(): summed_own, summed_prior = lax.psum((partial_own, partial_prior), 'mp')  17.9 us
    all_to_all x1, waiting for transfers between devices, on_device(): lax.all_to_all(grad_slots.astype(jnp.bfloat16), 'blk', split_axis=0, conc...  10.1 us
    dot_general x2, matrix products, contract_cols(): lax.dot_general(left, right, (((0,), (0,)), ((), ())), preferred_element_...  6.08 us
    all_to_all x1, starting transfers between devices, on_device(): lax.all_to_all(found_rows, 'blk', split_axis=0, concat_axis=0, tiled=True)  4.25 us
    dot_general x2, matrix products, contract_rows(): lax.dot_general(left, right, (((1,), (1,)), ((), ())), preferred_element_...  3.92 us
    unnamed x20, local copies, waits for them, and re-layouts  3.81 us
    sort x1, other arithmetic, on_device(): ordering = jnp.argsort(match_dev, stable=True)  3.77 us
  transfers between devices with their start and end apart: 6, of which 5 were waited for; matrix products, arithmetic and copies ran while one was open for 25% of the time, Pallas kernels for 0%

commit v1 on v0

v1 whole, which is shorter than its diff:
```python
import functools
import jax
import jax.numpy as jnp
from jax import lax
from jax.experimental import pallas as pl
from jax.experimental.pallas import tpu as pltpu
from jax.sharding import PartitionSpec as P

SCALE = 10.0
LANES = 128
BF16 = jnp.bfloat16
F32 = jnp.float32
I32 = jnp.int32


def shifted(value, axis, steps):
    count = lax.axis_size(axis)
    pairs = [(source, (source + steps) % count) for source in range(count)]
    return lax.ppermute(value, axis, pairs)


def dot_nt(left, right):
    return lax.dot_general(left, right, (((1,), (1,)), ((), ())), preferred_element_type=F32)


def dot_nn(left, right):
    return lax.dot_general(left, right, (((1,), (0,)), ((), ())), preferred_element_type=F32)


def dot_tn(left, right):
    return lax.dot_general(left, right, (((0,), (0,)), ((), ())), preferred_element_type=F32)


def iota(shape, dimension):
    return lax.broadcasted_iota(I32, shape, dimension)


def one_hot(condition):
    return jnp.where(condition, 1.0, 0.0).astype(BF16)


def split_digits(values):
    return (values >> 8).astype(F32), (values & 255).astype(F32)


def rank_kernel(blocks, per_peer, dev_ref, row_ref, want_ref, slot_ref):
    rows = dev_ref.shape[1]
    dev = dev_ref[...]
    chosen = iota((blocks, rows), 0) == dev
    member = one_hot(chosen)
    earlier = one_hot(iota((rows, rows), 0) < iota((rows, rows), 1))
    before = dot_nn(member, earlier)
    rank = jnp.sum(jnp.where(chosen, before, 0.0), axis=0, keepdims=True).astype(I32)
    slot_ref[...] = dev * per_peer + rank
    place = one_hot(iota((LANES, rows), 0) == rank)
    high, low = split_digits(row_ref[...])
    wanted = 256.0 * dot_nt(jnp.where(chosen, high, 0.0).astype(BF16), place)
    wanted = wanted + dot_nt(jnp.where(chosen, low, 0.0).astype(BF16), place)
    wanted = wanted.astype(I32)
    want_ref[:, 0, :] = wanted
    want_ref[1:, 1, :] = wanted[:-1]
    want_ref[:1, 1, :] = wanted[-1:]


def listed(blocks, per_peer, table, along_lanes):
    count = blocks * per_peer
    high, low = split_digits(table)
    high, low = high.astype(BF16), low.astype(BF16)
    if along_lanes:
        spread = one_hot(iota((LANES, count), 0) == iota((LANES, count), 1) % per_peer)
        values = 256.0 * dot_nn(high, spread) + dot_nn(low, spread)
        mine = iota((blocks, count), 0) == iota((blocks, count), 1) // per_peer
        return jnp.sum(jnp.where(mine, values, 0.0), axis=0, keepdims=True).astype(I32)
    spread = one_hot(iota((count, LANES), 1) == iota((count, LANES), 0) % per_peer)
    values = 256.0 * dot_nt(spread, high) + dot_nt(spread, low)
    mine = iota((count, blocks), 1) == iota((count, blocks), 0) // per_peer
    return jnp.sum(jnp.where(mine, values, 0.0), axis=1, keepdims=True).astype(I32)


def serve_kernel(blocks, per_peer, asked_ref, slot_ref, anchors_ref, partners_ref, send_ref):
    rows = anchors_ref.shape[0]
    asked = listed(blocks, per_peer, asked_ref[:, 0, :], False)
    found = dot_nn(one_hot(asked == iota((rows, rows), 1)), partners_ref[...]).astype(BF16)
    slot = slot_ref[...] + per_peer
    slot = jnp.where(slot >= rows, slot - rows, slot)
    ordered = dot_nn(one_hot(iota((rows, rows), 0) == slot), anchors_ref[...]).astype(BF16)
    for block in range(blocks):
        part = slice(block * per_peer, (block + 1) * per_peer)
        send_ref[block, :per_peer, :] = found[part]
        send_ref[block, per_peer:, :] = ordered[part]


def as_column(row):
    count = row.shape[1]
    diagonal = iota((count, count), 0) == iota((count, count), 1)
    return jnp.sum(jnp.where(diagonal, row, 0.0), axis=1, keepdims=True)


def own_kernel(
    anchors_ref, other_anchors_ref, partners_ref, other_partners_ref, lse_ref, anchor_acc_ref, partner_acc_ref,
    toward_ref, staying_ref,
):
    logits = dot_nt(anchors_ref[...], partners_ref[...]) + dot_nt(other_anchors_ref[...], other_partners_ref[...])
    weights = jnp.exp(SCALE * logits - as_column(lse_ref[...])).astype(BF16)
    staying = partner_acc_ref[...] + SCALE * dot_tn(weights, anchors_ref[...])
    staying_ref[...] = staying.astype(BF16)
    toward_ref[...] = anchor_acc_ref[...] + SCALE * dot_nn(weights, partners_ref[...])


def prior_kernel(
    anchors_ref, other_anchors_ref, previous_ref, other_even_ref, other_odd_ref, lse_ref, toward_ref,
    anchor_ref, partner_ref,
):
    other_previous = other_even_ref[...] + other_odd_ref[...]
    logits = dot_nt(anchors_ref[...], previous_ref[...]) + dot_nt(other_anchors_ref[...], other_previous)
    weights = jnp.exp(SCALE * logits - as_column(lse_ref[...])).astype(BF16)
    anchor_ref[...] = toward_ref[...] + SCALE * dot_nn(weights, previous_ref[...])
    partner_ref[...] = SCALE * dot_tn(weights, anchors_ref[...])


def final_kernel(
    blocks, per_peer, got_ref, asked_ref, slot_ref, anchor_ref, partner_ref, arrived_ref,
    anchor_out_ref, partner_out_ref,
):
    rows = anchor_ref.shape[0]
    width = anchor_ref.shape[1]
    fetched = jnp.concatenate([got_ref[block, :per_peer, :] for block in range(blocks)], axis=0)
    home = jnp.concatenate([got_ref[block, per_peer:, :] for block in range(blocks)], axis=0)
    pick = one_hot(iota((rows, rows), 0) == slot_ref[...])
    anchor_out_ref[...] = anchor_ref[...] - SCALE * dot_tn(pick, fetched)
    asked = listed(blocks, per_peer, asked_ref[:, 1, :], True)
    put = one_hot(iota((rows, rows), 0) == asked)
    partner_out_ref[...] = arrived_ref[...].astype(F32) + partner_ref[...] - SCALE * dot_nn(put, home)


def call(kernel, name, flops, outs, *operands):
    size = sum(value.size * value.dtype.itemsize for value in (*operands, *outs))
    return pl.pallas_call(
        kernel,
        out_shape=outs,
        name=name,
        cost_estimate=pl.CostEstimate(flops=flops, bytes_accessed=size, transcendentals=0),
        compiler_params=pltpu.CompilerParams(vmem_limit_bytes=40 * 1024 * 1024),
    )(*operands)


def on_device(anchors, partners, row_lse, anchor_acc, partner_acc, match_dev, match_row):
    rows, width = anchors.shape
    blocks = lax.axis_size("blk")
    per_peer = rows // blocks
    shape = jax.ShapeDtypeStruct
    cube = 2 * rows * rows * width

    want, slot = call(
        functools.partial(rank_kernel, blocks, per_peer), "rank", cube // 8,
        (shape((blocks, 2, LANES), I32), shape((1, rows), I32)),
        match_dev.reshape(1, rows), match_row.reshape(1, rows),
    )
    other_anchors = shifted(anchors, "mp", 1)
    other_partners = shifted(partners, "mp", 1)
    previous = shifted(partners, "blk", 1)
    asked = lax.all_to_all(want, "blk", split_axis=0, concat_axis=0, tiled=True)

    asked, previous, other_partners = lax.optimization_barrier((asked, previous, other_partners))

    across = [(2 * block + half, 2 * block + 1 - half) for block in range(0, blocks, 2) for half in range(2)]
    other_even = lax.ppermute(previous, ("blk", "mp"), across)
    other_odd = lax.ppermute(other_partners, "blk", [(block, block + 1) for block in range(0, blocks, 2)])

    (send,) = call(
        functools.partial(serve_kernel, blocks, per_peer), "serve", 2 * cube,
        (shape((blocks, 2 * per_peer, width), BF16),),
        asked, slot, anchors, partners,
    )
    got = lax.all_to_all(send, "blk", split_axis=0, concat_axis=0, tiled=True)

    lse_row = row_lse.reshape(1, rows)
    toward, staying = call(
        own_kernel, "own", 4 * cube,
        (shape((rows, width), F32), shape((rows, width), BF16)),
        anchors, other_anchors, partners, other_partners, lse_row, anchor_acc, partner_acc,
    )
    arrived = shifted(staying, "blk", 1)
    anchor_part, partner_part = call(
        prior_kernel, "prior", 4 * cube,
        (shape((rows, width), F32), shape((rows, width), F32)),
        anchors, other_anchors, previous, other_even, other_odd, lse_row, toward,
    )
    return call(
        functools.partial(final_kernel, blocks, per_peer), "final", 2 * cube,
        (shape((rows, width), F32), shape((rows, width), F32)),
        got, asked, slot, anchor_part, partner_part, arrived,
    )


def solution(mesh):
    return jax.shard_map(
        on_device,
        mesh=mesh,
        in_specs=(
            P("blk", "mp"),
            P("blk", "mp"),
            P("blk"),
            P("blk", "mp"),
            P("blk", "mp"),
            P("blk"),
            P("blk"),
        ),
        out_specs=(P("blk", "mp"), P("blk", "mp")),
        check_vma=False,
    )
```

time: 115 us -> 62.5 us (0.54)
  waiting for transfers between devices: 51.5 us -> 18 us
  between operations: 14.2 us -> 0.74 us
  blocking collectives: 0 us -> 12.2 us
  matrix products: 12 us -> 0 us
  other arithmetic: 9.04 us -> 0 us
  Pallas kernels: 0 us -> 6.97 us
  local copies, waits for them, and re-layouts: 15.7 us -> 10.7 us
    psum x1 -> x0, waiting for transfers between devices: 17.9 us -> none  [on_device(): summed_own, summed_prior = lax.psum((partial_own, partial_prior), 'mp')]
    all_to_all x3 -> x1, waiting for transfers between devices: 13.5 us -> 0.01 us  [on_device(): got = lax.all_to_all(send, 'blk', split_axis=0, concat_axis=0, tiled=True)]
    all_to_all x0 -> x1, blocking collectives: none -> 12.2 us  [on_device(): asked = lax.all_to_all(want, 'blk', split_axis=0, concat_axis=0, tiled=True)]
    dot_general x6 -> x0, matrix products: 12 us -> none  [the longest x2 6.08 us: contract_cols(): lax.dot_general(left, right, (((0,), (0,)), ((), ())), preferred_element_...]
    gather x3 -> x0, local copies, waits for them, and re-layouts: 7.43 us -> none  [the longest x1 3.48 us: on_device(): wanted = jnp.take(match_row, ordering).reshape(blocks, per_peer)]
    all_to_all x3 -> x1, starting transfers between devices: 11.6 us -> 4.54 us  [on_device(): got = lax.all_to_all(send, 'blk', split_axis=0, concat_axis=0, tiled=True)]
    pallas_call x0 -> x5, Pallas kernels: none -> 6.97 us  [call(): pl.pallas_call(kernel, out_shape=outs, name=name, cost_estimate=pl.CostEs...]
    unnamed x20 -> x34, local copies, waits for them, and re-layouts: 3.81 us -> 10.7 us
  transfers between devices with their start and end apart: 6 -> 7, of which waited for: 5 -> 3; matrix products, arithmetic and copies ran while one was open for 25% -> 0% of each run, Pallas kernels for 0% -> 5%
where the time goes in v1:
time: 62.5 us; the launch traced here: 61.7 us
  waiting for transfers between devices  18 us (29%)
  starting transfers between devices  13 us (21%)
  blocking collectives  12.2 us (20%)
  local copies, waits for them, and re-layouts  10.7 us (17%)
  Pallas kernels  6.97 us (11%)
  between operations  0.74 us (1%)
    ppermute x4, waiting for transfers between devices, shifted(): return lax.ppermute(value, axis, pairs)  16.2 us
    all_to_all x1, blocking collectives, on_device(): asked = lax.all_to_all(want, 'blk', split_axis=0, concat_axis=0, tiled=True)  12.2 us
    unnamed x34, local copies, waits for them, and re-layouts  10.7 us
    pallas_call x5, Pallas kernels, call(): pl.pallas_call(kernel, out_shape=outs, name=name, cost_estimate=pl.CostEs...  6.97 us
    ppermute x4, starting transfers between devices, shifted(): return lax.ppermute(value, axis, pairs)  4.93 us
    all_to_all x1, starting transfers between devices, on_device(): got = lax.all_to_all(send, 'blk', split_axis=0, concat_axis=0, tiled=True)  4.54 us
    ppermute x1, starting transfers between devices, on_device(): other_even = lax.ppermute(previous, ('blk', 'mp'), across)  2.21 us
    ppermute x1, waiting for transfers between devices, on_device(): other_even = lax.ppermute(previous, ('blk', 'mp'), across)  1.8 us
  transfers between devices with their start and end apart: 7, of which 3 were waited for; matrix products, arithmetic and copies ran while one was open for 0% of the time, Pallas kernels for 5%

profile of v1, /device:TPU:0, one launch (start us, length us, event | category | flops | bytes accessed | tf_op | source)
XLA Modules:
  0.0 61.7 jit_solution(14078589455203323511)
XLA Ops:
  0.6 0.0 copy-start.15
  0.6 0.5 collective-permute-start
  1.1 2.6 %collective-permute-start.1 = (bf16[512,512]{1,0:T(8,128)(2,1)}, bf16[512,512]{1,0:T(8,128)(2,1)S(1)}, u32[]{:S(2)}, u32[]{:S(2)}) collective-permute-start(bf16[512,512]{1,0:T(8,128)(2,1)} %partners_ref.3), channel_id=1, source_target_pairs={{0,1},{1,0},{2,3},{3,2},{4,5},{5,4},{6,7},{7,6},{8,9},{9,8},{10,11... | collective-permute-start | bytes 1572872 | tf_op jit(solution)/shard_map/ppermute | solution.py:19
  3.7 0.0 copy-done.15
  3.7 0.0 copy-start.16
  3.7 0.7 %copy-done.16 = s32[512]{0:T(512)S(1)} copy-done((s32[512]{0:T(512)S(1)}, s32[512]{0:T(512)}, u32[]{:S(2)}) %copy-start.16) | copy-done | bytes 2072
  4.4 0.4 rank.1
  4.8 12.2 %all_to_all.10.asked_ref = s32[16,2,128]{2,1,0:T(2,128)S(1)} all-to-all(s32[16,2,128]{2,1,0:T(2,128)S(1)} %get-tuple-element.11), channel_id=1, replica_groups=mesh['blk'=16,'mp'=2] {'blk'}, dimensions={0} | all-to-all | bytes 32768 | tf_op jit(solution)/shard_map/all_to_all | solution.py:162
  17.0 0.0 collective-permute-done.previous_ref
  17.0 0.0 copy-start.13
  17.0 0.0 collective-permute-done.1.other_partners_ref
  17.0 0.8 %copy-done.13 = bf16[512,512]{1,0:T(8,128)(2,1)} copy-done((bf16[512,512]{1,0:T(8,128)(2,1)}, bf16[512,512]{1,0:T(8,128)(2,1)S(1)}, u32[]{:S(2)}) %copy-start.13) | copy-done | bytes 524312
  17.8 0.0 copy-start.10
  17.8 0.8 %copy-done.10 = bf16[512,512]{1,0:T(8,128)(2,1)} copy-done((bf16[512,512]{1,0:T(8,128)(2,1)}, bf16[512,512]{1,0:T(8,128)(2,1)S(1)}, u32[]{:S(2)}) %copy-start.10) | copy-done | bytes 524312
  18.6 0.0 copy-start
  18.6 1.0 %copy-done = bf16[512,512]{1,0:T(8,128)(2,1)S(1)} copy-done((bf16[512,512]{1,0:T(8,128)(2,1)S(1)}, bf16[512,512]{1,0:T(8,128)(2,1)}, u32[]{:S(2)}) %copy-start) | copy-done | bytes 524312
  19.7 0.0 copy-start.2
  19.7 1.0 %copy-done.2 = bf16[512,512]{1,0:T(8,128)(2,1)S(1)} copy-done((bf16[512,512]{1,0:T(8,128)(2,1)S(1)}, bf16[512,512]{1,0:T(8,128)(2,1)}, u32[]{:S(2)}) %copy-start.2) | copy-done | bytes 524312
  20.7 0.0 copy-start.12
  20.7 1.9 %serve.1 = bf16[16,64,512]{2,1,0:T(8,128)(2,1)} custom-call(s32[16,2,128]{2,1,0:T(2,128)S(1)} %all_to_all.10.asked_ref, s32[1,512]{1,0:T(1,128)S(1)} %get-tuple-element.13.slot_ref, bf16[512,512]{1,0:T(8,128)(2,1)S(1)} %copy-done.2, bf16[512,512]{1,0:T(8,128)(2,1)S(1)} %copy-done), custom_call_target="tpu_custom_call" | custom-call | flops 536870912 | bytes 2115584 | tf_op jit(solution)/shard_map/serve/pallas_call | solution.py:138
  22.6 0.0 copy-start.3
  22.6 0.0 copy-start.1
  22.6 4.5 %all-to-all-start.1 = ((bf16[16,64,512]{2,1,0:T(8,128)(2,1)}), bf16[16,64,512]{2,1,0:T(8,128)(2,1)S(1)}, u32[]{:S(2)}, u32[]{:S(2)}) async-start(bf16[16,64,512]{2,1,0:T(8,128)(2,1)} %serve.1), calls=%async_computation.1 | async-start | bytes 2097152 | tf_op jit(solution)/shard_map/all_to_all | solution.py:175
  27.2 0.0 copy-done.3
  27.2 1.8 %collective-permute-start.2 = (bf16[512,512]{1,0:T(8,128)(2,1)S(1)}, bf16[512,512]{1,0:T(8,128)(2,1)S(1)}, u32[]{:S(2)}, u32[]{:S(2)}) collective-permute-start(bf16[512,512]{1,0:T(8,128)(2,1)S(1)} %copy-done.3), channel_id=1, source_target_pairs={{0,1},{1,0},{2,3},{3,2},{4,5},{5,4},{6,7},{7,6},{8,9},{9,8},{10,11... | collective-permute-start | bytes 1572872 | tf_op jit(solution)/shard_map/ppermute | solution.py:19
  29.0 2.2 %collective-permute-start.3 = (bf16[512,512]{1,0:T(8,128)(2,1)}, bf16[512,512]{1,0:T(8,128)(2,1)S(1)}, u32[]{:S(2)}, u32[]{:S(2)}) collective-permute-start(bf16[512,512]{1,0:T(8,128)(2,1)} %copy-done.13), channel_id=1, source_target_pairs={{0,1},{1,0},{4,5},{5,4},{8,9},{9,8},{12,13},{13,12},{16,17},{17,16... | collective-permute-start | bytes 1572872 | tf_op jit(solution)/shard_map/ppermute | solution.py:167
  31.2 1.3 %collective-permute-start.4 = (bf16[512,512]{1,0:T(8,128)(2,1)}, bf16[512,512]{1,0:T(8,128)(2,1)S(1)}, u32[]{:S(2)}, u32[]{:S(2)}) collective-permute-start(bf16[512,512]{1,0:T(8,128)(2,1)} %copy-done.10), channel_id=1, source_target_pairs={{0,2},{4,6},{8,10},{12,14},{16,18},{20,22},{24,26},{28,30},{1,3},{... | collective-permute-start | bytes 1572872 | tf_op jit(solution)/shard_map/ppermute | solution.py:168
  32.5 9.0 %collective-permute-done.2.other_anchors_ref = bf16[512,512]{1,0:T(8,128)(2,1)S(1)} collective-permute-done((bf16[512,512]{1,0:T(8,128)(2,1)S(1)}, bf16[512,512]{1,0:T(8,128)(2,1)S(1)}, u32[]{:S(2)}, u32[]{:S(2)}) %collective-permute-start.2) | collective-permute-done | bytes 524320 | tf_op jit(solution)/shard_map/ppermute | solution.py:19
  41.5 0.0 copy-done.12
  41.5 0.0 copy-done.1
  41.5 0.0 copy-done.6
  41.5 0.0 copy-start.7
  41.5 1.2 %copy-done.7 = f32[512,512]{1,0:T(8,128)S(1)} copy-done((f32[512,512]{1,0:T(8,128)S(1)}, f32[512,512]{1,0:T(8,128)}, u32[]{:S(2)}) %copy-start.7) | copy-done | bytes 1048600
  42.7 1.0 %copy-done.11 = bf16[512,512]{1,0:T(8,128)(2,1)S(1)} copy-done((bf16[512,512]{1,0:T(8,128)(2,1)S(1)}, bf16[512,512]{1,0:T(8,128)(2,1)}, u32[]{:S(2)}) %copy-start.11) | copy-done | bytes 524312
  43.8 1.5 %own.1 = (f32[512,512]{1,0:T(8,128)S(1)}, bf16[512,512]{1,0:T(8,128)(2,1)S(1)}) custom-call(bf16[512,512]{1,0:T(8,128)(2,1)S(1)} %copy-done.3, bf16[512,512]{1,0:T(8,128)(2,1)S(1)} %collective-permute-done.2.other_anchors_ref, bf16[512,512]{1,0:T(8,128)(2,1)S(1)} %copy-done.1, bf16[512,512]{1,0:T(8,128)(2,1)S(1)} %copy-done.11, f32[1,512]{1,0:T(1,128)S(1)} %bitcast.3, ...), custom_call_target="tpu_custom_call" | custom-call | flops 1073741824 | bytes 5769216 | tf_op jit(solution)/shard_map/own/pallas_call | solution.py:138
  45.3 0.1 collective-permute-start.5
  45.3 1.8 %collective-permute-done.3.other_even_ref = bf16[512,512]{1,0:T(8,128)(2,1)S(1)} collective-permute-done((bf16[512,512]{1,0:T(8,128)(2,1)}, bf16[512,512]{1,0:T(8,128)(2,1)S(1)}, u32[]{:S(2)}, u32[]{:S(2)}) %collective-permute-start.3) | collective-permute-done | bytes 524320 | tf_op jit(solution)/shard_map/ppermute | solution.py:167
  47.1 0.0 collective-permute-done.4.other_odd_ref
  47.1 0.0 copy-done.14
  47.1 1.4 %prior.1 = (f32[512,512]{1,0:T(8,128)S(1)}, f32[512,512]{1,0:T(8,128)S(1)}) custom-call(bf16[512,512]{1,0:T(8,128)(2,1)S(1)} %copy-done.3, bf16[512,512]{1,0:T(8,128)(2,1)S(1)} %collective-permute-done.2.other_anchors_ref, bf16[512,512]{1,0:T(8,128)(2,1)S(1)} %copy-done.14, bf16[512,512]{1,0:T(8,128)(2,1)S(1)} %collective-permute-done.3.other_even_ref, ...), custom_call_target="tpu_custom_call" | custom-call | flops 1073741824 | bytes 5769216 | tf_op jit(solution)/shard_map/prior/pallas_call | solution.py:138
  48.5 0.0 copy-start.4
  48.5 1.0 %copy-done.4 = f32[512,512]{1,0:T(8,128)} copy-done((f32[512,512]{1,0:T(8,128)}, f32[512,512]{1,0:T(8,128)S(1)}, u32[]{:S(2)}) %copy-start.4) | copy-done | bytes 1048600
  49.5 7.2 %collective-permute-done.5.arrived_ref = bf16[512,512]{1,0:T(8,128)(2,1)S(1)} collective-permute-done((bf16[512,512]{1,0:T(8,128)(2,1)S(1)}, bf16[512,512]{1,0:T(8,128)(2,1)S(1)}, u32[]{:S(2)}, u32[]{:S(2)}) %collective-permute-start.5) | collective-permute-done | bytes 524320 | tf_op jit(solution)/shard_map/ppermute | solution.py:19
  56.7 0.8 %copy-done.8 = bf16[512,512]{1,0:T(8,128)(2,1)} copy-done((bf16[512,512]{1,0:T(8,128)(2,1)}, bf16[512,512]{1,0:T(8,128)(2,1)S(1)}, u32[]{:S(2)}) %copy-start.8) | copy-done | bytes 524312
  57.5 0.0 all-to-all-done.1.got_ref
  57.5 1.2 %copy-done.5 = f32[512,512]{1,0:T(8,128)S(1)} copy-done((f32[512,512]{1,0:T(8,128)S(1)}, f32[512,512]{1,0:T(8,128)}, u32[]{:S(2)}) %copy-start.5) | copy-done | bytes 1048600
  58.8 1.0 %copy-done.9 = bf16[512,512]{1,0:T(8,128)(2,1)S(1)} copy-done((bf16[512,512]{1,0:T(8,128)(2,1)S(1)}, bf16[512,512]{1,0:T(8,128)(2,1)}, u32[]{:S(2)}) %copy-start.9) | copy-done | bytes 524312
  59.8 1.9 %final.1 = (f32[512,512]{1,0:T(8,128)}, f32[512,512]{1,0:T(8,128)}) custom-call(bf16[16,64,512]{2,1,0:T(8,128)(2,1)S(1)} %all-to-all-done.1.got_ref, s32[16,2,128]{2,1,0:T(2,128)S(1)} %all_to_all.10.asked_ref, s32[1,512]{1,0:T(1,128)S(1)} %get-tuple-element.13.slot_ref, f32[512,512]{1,0:T(8,128)S(1)} %get-tuple-element.17.anchor_ref, ...), custom_call_target="tpu_custom_call" | custom-call | flops 536870912 | bytes 5785600 | tf_op jit(solution)/shard_map/final/pallas_call | solution.py:138
  (6 shorter events, 0.0 us)
Async XLA Ops:
  0.6 3.1 %copy-start.15 = (s32[512]{0:T(512)S(1)}, s32[512]{0:T(512)}, u32[]{:S(2)}) copy-start(s32[512]{0:T(512)} %param.12) | copy-start | bytes 6148
  0.6 16.4 %collective-permute-start = (bf16[512,512]{1,0:T(8,128)(2,1)}, bf16[512,512]{1,0:T(8,128)(2,1)S(1)}, u32[]{:S(2)}, u32[]{:S(2)}) collective-permute-start(bf16[512,512]{1,0:T(8,128)(2,1)} %partners_ref.3), channel_id=1, source_target_pairs={{0,2},{2,4},{4,6},{6,8},{8,10},{10,12},{12,14},{14,16},{16,18},{18... | collective-permute-start | bytes 1572872 | tf_op jit(solution)/shard_map/ppermute | solution.py:19
  1.1 15.9 %collective-permute-start.1 = (bf16[512,512]{1,0:T(8,128)(2,1)}, bf16[512,512]{1,0:T(8,128)(2,1)S(1)}, u32[]{:S(2)}, u32[]{:S(2)}) collective-permute-start(bf16[512,512]{1,0:T(8,128)(2,1)} %partners_ref.3), channel_id=1, source_target_pairs={{0,1},{1,0},{2,3},{3,2},{4,5},{5,4},{6,7},{7,6},{8,9},{9,8},{10,11... | collective-permute-start | bytes 1572872 | tf_op jit(solution)/shard_map/ppermute | solution.py:19
  3.7 0.7 %copy-start.16 = (s32[512]{0:T(512)S(1)}, s32[512]{0:T(512)}, u32[]{:S(2)}) copy-start(s32[512]{0:T(512)} %param.13) | copy-start | bytes 6148
  17.0 0.8 %copy-start.13 = (bf16[512,512]{1,0:T(8,128)(2,1)}, bf16[512,512]{1,0:T(8,128)(2,1)S(1)}, u32[]{:S(2)}) copy-start(bf16[512,512]{1,0:T(8,128)(2,1)S(1)} %collective-permute-done.previous_ref) | copy-start | bytes 1572868
  17.8 0.8 %copy-start.10 = (bf16[512,512]{1,0:T(8,128)(2,1)}, bf16[512,512]{1,0:T(8,128)(2,1)S(1)}, u32[]{:S(2)}) copy-start(bf16[512,512]{1,0:T(8,128)(2,1)S(1)} %collective-permute-done.1.other_partners_ref) | copy-start | bytes 1572868
  18.6 1.0 %copy-start = (bf16[512,512]{1,0:T(8,128)(2,1)S(1)}, bf16[512,512]{1,0:T(8,128)(2,1)}, u32[]{:S(2)}) copy-start(bf16[512,512]{1,0:T(8,128)(2,1)} %partners_ref.3) | copy-start | bytes 1572868
  19.7 1.0 %copy-start.2 = (bf16[512,512]{1,0:T(8,128)(2,1)S(1)}, bf16[512,512]{1,0:T(8,128)(2,1)}, u32[]{:S(2)}) copy-start(bf16[512,512]{1,0:T(8,128)(2,1)} %anchors_ref.5) | copy-start | bytes 1572868
  20.7 20.8 %copy-start.12 = (f32[512]{0:T(512)S(1)}, f32[512]{0:T(512)}, u32[]{:S(2)}) copy-start(f32[512]{0:T(512)} %param.9) | copy-start | bytes 6148
  22.6 4.6 %copy-start.3 = (bf16[512,512]{1,0:T(8,128)(2,1)S(1)}, bf16[512,512]{1,0:T(8,128)(2,1)}, u32[]{:S(2)}) copy-start(bf16[512,512]{1,0:T(8,128)(2,1)} %anchors_ref.5) | copy-start | bytes 1572868
  22.6 18.9 %copy-start.1 = (bf16[512,512]{1,0:T(8,128)(2,1)S(1)}, bf16[512,512]{1,0:T(8,128)(2,1)}, u32[]{:S(2)}) copy-start(bf16[512,512]{1,0:T(8,128)(2,1)} %partners_ref.3) | copy-start | bytes 1572868
  22.6 18.9 %copy-start.6 = (f32[512,512]{1,0:T(8,128)S(1)}, f32[512,512]{1,0:T(8,128)}, u32[]{:S(2)}) copy-start(f32[512,512]{1,0:T(8,128)} %anchor_acc_ref.1) | copy-start | bytes 3145732
  22.6 34.9 %all-to-all-start.1 = ((bf16[16,64,512]{2,1,0:T(8,128)(2,1)}), bf16[16,64,512]{2,1,0:T(8,128)(2,1)S(1)}, u32[]{:S(2)}, u32[]{:S(2)}) async-start(bf16[16,64,512]{2,1,0:T(8,128)(2,1)} %serve.1), calls=%async_computation.1 | async-start | bytes 2097152 | tf_op jit(solution)/shard_map/all_to_all | solution.py:175
  27.2 14.3 %collective-permute-start.2 = (bf16[512,512]{1,0:T(8,128)(2,1)S(1)}, bf16[512,512]{1,0:T(8,128)(2,1)S(1)}, u32[]{:S(2)}, u32[]{:S(2)}) collective-permute-start(bf16[512,512]{1,0:T(8,128)(2,1)S(1)} %copy-done.3), channel_id=1, source_target_pairs={{0,1},{1,0},{2,3},{3,2},{4,5},{5,4},{6,7},{7,6},{8,9},{9,8},{10,11... | collective-permute-start | bytes 1572872 | tf_op jit(solution)/shard_map/ppermute | solution.py:19
  29.0 18.2 %collective-permute-start.3 = (bf16[512,512]{1,0:T(8,128)(2,1)}, bf16[512,512]{1,0:T(8,128)(2,1)S(1)}, u32[]{:S(2)}, u32[]{:S(2)}) collective-permute-start(bf16[512,512]{1,0:T(8,128)(2,1)} %copy-done.13), channel_id=1, source_target_pairs={{0,1},{1,0},{4,5},{5,4},{8,9},{9,8},{12,13},{13,12},{16,17},{17,16... | collective-permute-start | bytes 1572872 | tf_op jit(solution)/shard_map/ppermute | solution.py:167
  31.2 15.9 %collective-permute-start.4 = (bf16[512,512]{1,0:T(8,128)(2,1)}, bf16[512,512]{1,0:T(8,128)(2,1)S(1)}, u32[]{:S(2)}, u32[]{:S(2)}) collective-permute-start(bf16[512,512]{1,0:T(8,128)(2,1)} %copy-done.10), channel_id=1, source_target_pairs={{0,2},{4,6},{8,10},{12,14},{16,18},{20,22},{24,26},{28,30},{1,3},{... | collective-permute-start | bytes 1572872 | tf_op jit(solution)/shard_map/ppermute | solution.py:168
  41.5 1.2 %copy-start.7 = (f32[512,512]{1,0:T(8,128)S(1)}, f32[512,512]{1,0:T(8,128)}, u32[]{:S(2)}) copy-start(f32[512,512]{1,0:T(8,128)} %partner_acc_ref.1) | copy-start | bytes 3145732
  42.7 1.0 %copy-start.11 = (bf16[512,512]{1,0:T(8,128)(2,1)S(1)}, bf16[512,512]{1,0:T(8,128)(2,1)}, u32[]{:S(2)}) copy-start(bf16[512,512]{1,0:T(8,128)(2,1)} %copy-done.10) | copy-start | bytes 1572868
  43.8 3.3 %copy-start.14 = (bf16[512,512]{1,0:T(8,128)(2,1)S(1)}, bf16[512,512]{1,0:T(8,128)(2,1)}, u32[]{:S(2)}) copy-start(bf16[512,512]{1,0:T(8,128)(2,1)} %copy-done.13) | copy-start | bytes 1572868
  45.3 11.5 %collective-permute-start.5 = (bf16[512,512]{1,0:T(8,128)(2,1)S(1)}, bf16[512,512]{1,0:T(8,128)(2,1)S(1)}, u32[]{:S(2)}, u32[]{:S(2)}) collective-permute-start(bf16[512,512]{1,0:T(8,128)(2,1)S(1)} %get-tuple-element.19), channel_id=1, source_target_pairs={{0,2},{2,4},{4,6},{6,8},{8,10},{10,12},{12,14},{14,16},{16,18},{18... | collective-permute-start | bytes 1572872 | tf_op jit(solution)/shard_map/ppermute | solution.py:19
  48.5 1.0 %copy-start.4 = (f32[512,512]{1,0:T(8,128)}, f32[512,512]{1,0:T(8,128)S(1)}, u32[]{:S(2)}) copy-start(f32[512,512]{1,0:T(8,128)S(1)} %get-tuple-element.18.partner_ref) | copy-start | bytes 3145732
  56.7 0.8 %copy-start.8 = (bf16[512,512]{1,0:T(8,128)(2,1)}, bf16[512,512]{1,0:T(8,128)(2,1)S(1)}, u32[]{:S(2)}) copy-start(bf16[512,512]{1,0:T(8,128)(2,1)S(1)} %collective-permute-done.5.arrived_ref) | copy-start | bytes 1572868
  57.5 1.2 %copy-start.5 = (f32[512,512]{1,0:T(8,128)S(1)}, f32[512,512]{1,0:T(8,128)}, u32[]{:S(2)}) copy-start(f32[512,512]{1,0:T(8,128)} %copy-done.4) | copy-start | bytes 3145732
  58.7 1.0 %copy-start.9 = (bf16[512,512]{1,0:T(8,128)(2,1)S(1)}, bf16[512,512]{1,0:T(8,128)(2,1)}, u32[]{:S(2)}) copy-start(bf16[512,512]{1,0:T(8,128)(2,1)} %copy-done.8) | copy-start | bytes 1572868

commit v2 on v1

v2 whole, which is shorter than its diff:
```python
import functools
import jax
import jax.numpy as jnp
from jax import lax
from jax.experimental import pallas as pl
from jax.experimental.pallas import tpu as pltpu
from jax.sharding import PartitionSpec as P

SCALE = 10.0
LANES = 128
EXTRA = 16
COST = dict(rank=1, serve=0, own=16, prior=16, final=8)
MID = 40_000_000
SERVE = 63_400_000
BF16 = jnp.bfloat16
F32 = jnp.float32
I32 = jnp.int32


def shifted(value, axis, steps):
    count = lax.axis_size(axis)
    pairs = [(source, (source + steps) % count) for source in range(count)]
    return lax.ppermute(value, axis, pairs)


def dot_nt(left, right):
    return lax.dot_general(left, right, (((1,), (1,)), ((), ())), preferred_element_type=F32)


def dot_nn(left, right):
    return lax.dot_general(left, right, (((1,), (0,)), ((), ())), preferred_element_type=F32)


def dot_tn(left, right):
    return lax.dot_general(left, right, (((0,), (0,)), ((), ())), preferred_element_type=F32)


def iota(shape, dimension):
    return lax.broadcasted_iota(I32, shape, dimension)


def one_hot(condition):
    return jnp.where(condition, 1.0, 0.0).astype(BF16)


def split_digits(values):
    return (values >> 8).astype(F32), (values & 255).astype(F32)


def begin(*pairs):
    copies = [pltpu.make_async_copy(*pair) for pair in pairs]
    for copy in copies:
        copy.start()
    return copies


def rank_kernel(
    blocks, per_peer, padded, dev_hbm, row_hbm, anchors_hbm, send_hbm, slot_ref,
    dev_ref, row_ref, anchors_ref, ordered_ref, digits_ref, packed_ref, sems,
):
    copies = begin(
        (dev_hbm, dev_ref, sems.at[0]), (row_hbm, row_ref, sems.at[1]), (anchors_hbm, anchors_ref, sems.at[2])
    )
    rows, width = anchors_ref.shape
    earlier = one_hot(iota((rows, rows), 0) < iota((rows, rows), 1))
    digits_ref[...] = jnp.zeros_like(digits_ref)
    copies[0].wait()
    dev = dev_ref[...].reshape(1, rows)
    chosen = iota((blocks, rows), 0) == dev
    before = dot_nn(one_hot(chosen), earlier)
    rank = jnp.sum(jnp.where(chosen, before, 0.0), axis=0, keepdims=True).astype(I32)
    slot_ref[...] = dev * per_peer + rank
    after = jnp.where(dev == blocks - 1, 0, dev + 1)
    pick = one_hot(iota((blocks * padded, rows), 0) == after * padded + rank)
    copies[2].wait()
    ordered = dot_nn(pick, anchors_ref[...]).astype(BF16)
    ordered_ref[...] = ordered.reshape(ordered_ref.shape)
    outgoing = begin(*[
        (
            ordered_ref.at[:, :, pl.ds(part * LANES, LANES)],
            send_hbm.at[:, pl.ds(part * padded, padded), :],
            sems.at[3 + part],
        )
        for part in range(width // LANES)
    ])
    place = one_hot(iota((LANES, rows), 0) == rank)
    copies[1].wait()
    for digit, values in enumerate(split_digits(row_ref[...].reshape(1, rows))):
        wanted = dot_nt(jnp.where(chosen, values, 0.0).astype(BF16), place)
        digits_ref[:, digit, :] = wanted
        digits_ref[1:, 2 + digit, :] = wanted[:-1]
        digits_ref[:1, 2 + digit, :] = wanted[-1:]
    packed_ref[...] = digits_ref[...].astype(BF16)
    outgoing += begin((packed_ref, send_hbm.at[:, pl.ds(width // LANES * padded, EXTRA), :], sems.at[3 + width // LANES]))
    for copy in outgoing:
        copy.wait()


def listed_column(blocks, per_peer, high, low):
    count = blocks * per_peer
    spread = one_hot(iota((count, LANES), 1) == iota((count, LANES), 0) % per_peer)
    values = 256.0 * dot_nt(spread, high) + dot_nt(spread, low)
    mine = iota((count, blocks), 1) == iota((count, blocks), 0) // per_peer
    return jnp.sum(jnp.where(mine, values, 0.0), axis=1, keepdims=True).astype(I32)


def listed_row(blocks, per_peer, padded, high, low):
    count = blocks * padded
    place = iota((LANES, count), 1) % padded
    spread = one_hot(iota((LANES, count), 0) == place)
    values = 256.0 * dot_nn(high, spread) + dot_nn(low, spread)
    mine = iota((blocks, count), 0) == iota((blocks, count), 1) // padded
    asked = jnp.sum(jnp.where(mine, values, 0.0), axis=0, keepdims=True).astype(I32)
    return jnp.where(iota((1, count), 1) % padded < per_peer, asked, -1)


def serve_kernel(blocks, per_peer, got_hbm, partners_hbm, send_ref, packed_ref, partners_ref, sems):
    rows, width = partners_ref.shape
    table, fetch = begin(
        (got_hbm.at[:, pl.ds(got_hbm.shape[1] - EXTRA, EXTRA), :], packed_ref, sems.at[0]),
        (partners_hbm, partners_ref, sems.at[1]),
    )
    table.wait()
    digits = packed_ref[...].astype(F32)
    asked = listed_column(blocks, per_peer, digits[:, 0, :].astype(BF16), digits[:, 1, :].astype(BF16))
    pick = one_hot(asked == iota((rows, rows), 1))
    fetch.wait()
    send_ref[...] = dot_nn(pick, partners_ref[...]).astype(BF16)


def as_column(row):
    count = row.shape[1]
    diagonal = iota((count, count), 0) == iota((count, count), 1)
    return jnp.sum(jnp.where(diagonal, row, 0.0), axis=1, keepdims=True)


def own_kernel(
    anchors_ref, other_anchors_ref, partners_ref, other_partners_ref, lse_ref, anchor_acc_ref, partner_acc_ref,
    toward_ref, staying_ref,
):
    logits = dot_nt(anchors_ref[...], partners_ref[...]) + dot_nt(other_anchors_ref[...], other_partners_ref[...])
    weights = jnp.exp(SCALE * logits - as_column(lse_ref[...])).astype(BF16)
    staying = partner_acc_ref[...] + SCALE * dot_tn(weights, anchors_ref[...])
    staying_ref[...] = staying.astype(BF16)
    toward_ref[...] = anchor_acc_ref[...] + SCALE * dot_nn(weights, partners_ref[...])


def prior_kernel(
    blocks, per_peer, padded,
    anchors_ref, other_anchors_ref, previous_ref, other_even_ref, other_odd_ref, lse_ref, toward_ref, got_hbm,
    anchor_ref, partner_ref, home_ref, packed_ref, sems,
):
    rows, width = anchors_ref.shape
    copies = begin(
        (got_hbm.at[:, pl.ds(width // LANES * padded, EXTRA), :], packed_ref, sems.at[0]),
        *[
            (
                got_hbm.at[:, pl.ds(part * padded, padded), :],
                home_ref.at[:, :, pl.ds(part * LANES, LANES)],
                sems.at[1 + part],
            )
            for part in range(width // LANES)
        ],
    )
    other_previous = other_even_ref[...] + other_odd_ref[...]
    logits = dot_nt(anchors_ref[...], previous_ref[...]) + dot_nt(other_anchors_ref[...], other_previous)
    weights = jnp.exp(SCALE * logits - as_column(lse_ref[...])).astype(BF16)
    anchor_ref[...] = toward_ref[...] + SCALE * dot_nn(weights, previous_ref[...])
    for copy in copies:
        copy.wait()
    digits = packed_ref[...].astype(F32)
    asked = listed_row(blocks, per_peer, padded, digits[:, 2, :].astype(BF16), digits[:, 3, :].astype(BF16))
    put = one_hot(iota((rows, blocks * padded), 0) == asked)
    home = dot_nn(put, home_ref[...].reshape(blocks * padded, width))
    partner_ref[...] = SCALE * dot_tn(weights, anchors_ref[...]) - SCALE * home


def final_kernel(fetched_hbm, slot_hbm, anchor_hbm, out_ref, fetched_ref, slot_ref, anchor_ref, sems):
    rows, width = anchor_ref.shape
    copies = begin(
        (slot_hbm, slot_ref, sems.at[0]), (fetched_hbm, fetched_ref, sems.at[1]), (anchor_hbm, anchor_ref, sems.at[2])
    )
    copies[0].wait()
    slot = as_column(slot_ref[...].astype(F32)).astype(I32)
    pick = one_hot(iota((rows, rows), 1) == slot)
    copies[1].wait()
    copies[2].wait()
    out_ref[...] = anchor_ref[...] - SCALE * dot_nn(pick, fetched_ref[...])


def call(kernel, name, flops, outs, operands, spaces=None, out_space=None, scratch=(), aliases=None, limit=63_400_000):
    size = sum(value.size * value.dtype.itemsize for value in (*operands, *outs))
    spaces = spaces or "v" * len(operands)
    specs = [pl.BlockSpec(memory_space={"v": pltpu.VMEM, "h": pltpu.HBM}[space]) for space in spaces]
    return pl.pallas_call(
        kernel,
        out_shape=outs,
        name=name,
        in_specs=specs,
        out_specs=tuple(pl.BlockSpec(memory_space=space) for space in out_space or (pltpu.VMEM,) * len(outs)),
        scratch_shapes=list(scratch),
        input_output_aliases=aliases or {},
        cost_estimate=pl.CostEstimate(flops=flops, bytes_accessed=size, transcendentals=0),
        compiler_params=pltpu.CompilerParams(vmem_limit_bytes=limit),
    )(*operands)


def on_device(anchors, partners, row_lse, anchor_acc, partner_acc, match_dev, match_row):
    rows, width = anchors.shape
    blocks = lax.axis_size("blk")
    per_peer = rows // blocks
    shape = jax.ShapeDtypeStruct
    dma = pltpu.SemaphoreType.DMA
    cube = 2 * rows * rows * width

    assert per_peer <= LANES and width % LANES == 0
    padded = -(-per_peer // 16) * 16
    tall = width // LANES * padded + EXTRA

    send, slot = call(
        functools.partial(rank_kernel, blocks, per_peer, padded), "rank", COST["rank"] * cube // 4,
        (shape((blocks, tall, LANES), BF16), shape((1, rows), I32)),
        (match_dev, match_row, anchors), spaces="hhh", out_space=(pltpu.HBM, pltpu.VMEM),
        scratch=(
            pltpu.VMEM((rows,), I32), pltpu.VMEM((rows,), I32), pltpu.VMEM((rows, width), BF16),
            pltpu.VMEM((blocks, padded, width), BF16), pltpu.VMEM((blocks, EXTRA, LANES), F32),
            pltpu.VMEM((blocks, EXTRA, LANES), BF16), dma((4 + width // LANES,)),
        ),
    )
    got = lax.all_to_all(send, "blk", split_axis=0, concat_axis=0, tiled=True)

    other_anchors = shifted(anchors, "mp", 1)
    other_partners = shifted(partners, "mp", 1)
    got, ring_partners = lax.optimization_barrier((got, partners))
    previous = shifted(ring_partners, "blk", 1)
    got, other_anchors = lax.optimization_barrier((got, other_anchors))
    across = [(2 * block + half, 2 * block + 1 - half) for block in range(0, blocks, 2) for half in range(2)]
    other_even = lax.ppermute(previous, ("blk", "mp"), across)
    other_odd = lax.ppermute(other_partners, "blk", [(block, block + 1) for block in range(0, blocks, 2)])

    (found,) = call(
        functools.partial(serve_kernel, blocks, per_peer), "serve", COST["serve"] * cube // 4,
        (shape((rows, width), BF16),),
        (got, partners), spaces="hh", limit=SERVE,
        scratch=(pltpu.VMEM((blocks, EXTRA, LANES), BF16), pltpu.VMEM((rows, width), BF16), dma((2,))),
    )
    fetched = lax.all_to_all(
        found.reshape(blocks, per_peer, width), "blk", split_axis=0, concat_axis=0, tiled=True
    ).reshape(rows, width)

    lse_row = row_lse.reshape(1, rows)
    toward, staying = call(
        own_kernel, "own", COST["own"] * cube // 4,
        (shape((rows, width), F32), shape((rows, width), BF16)),
        (anchors, other_anchors, partners, other_partners, lse_row, anchor_acc, partner_acc), limit=MID,
    )
    arrived = shifted(staying, "blk", 1)
    anchor_part, partner_part = call(
        functools.partial(prior_kernel, blocks, per_peer, padded), "prior", COST["prior"] * cube // 4,
        (shape((rows, width), F32), shape((rows, width), F32)),
        (anchors, other_anchors, previous, other_even, other_odd, lse_row, toward, got), spaces="vvvvvvvh", limit=MID,
        scratch=(
            pltpu.VMEM((blocks, padded, width), BF16), pltpu.VMEM((blocks, EXTRA, LANES), BF16),
            dma((1 + width // LANES,)),
        ),
    )
    partner_out = arrived.astype(F32) + partner_part
    (anchor_grad,) = call(
        final_kernel, "final", COST["final"] * cube // 4,
        (shape((rows, width), F32),),
        (fetched, slot, anchor_part), spaces="hhh",
        scratch=(
            pltpu.VMEM((rows, width), BF16), pltpu.VMEM(slot.shape, I32), pltpu.VMEM((rows, width), F32), dma((3,)),
        ),
    )
    return anchor_grad, partner_out


def solution(mesh):
    return jax.shard_map(
        on_device,
        mesh=mesh,
        in_specs=(
            P("blk", "mp"),
            P("blk", "mp"),
            P("blk"),
            P("blk", "mp"),
            P("blk", "mp"),
            P("blk"),
            P("blk"),
        ),
        out_specs=(P("blk", "mp"), P("blk", "mp")),
        check_vma=False,
    )
```

time: 62.5 us -> 59.4 us (0.950)
  blocking collectives: 12.2 us -> 0 us
  local copies, waits for them, and re-layouts: 10.7 us -> 3.01 us
  Pallas kernels: 6.97 us -> 14.4 us
  starting transfers between devices: 13 us -> 19.8 us
  waiting for transfers between devices: 18 us -> 19.7 us
  other arithmetic: 0 us -> 1.15 us
    ppermute x4, waiting for transfers between devices: 16.2 us -> 2.8 us  [shifted(): return lax.ppermute(value, axis, pairs)]
    all_to_all x1, waiting for transfers between devices: 0.01 us -> 13.4 us  [on_device(): got = lax.all_to_all(send, 'blk', split_axis=0, concat_axis=0, tiled=True)]
    all_to_all x1 -> x0, blocking collectives: 12.2 us -> none  [on_device(): asked = lax.all_to_all(want, 'blk', split_axis=0, concat_axis=0, tiled=True)]
    unnamed x34 -> x18, local copies, waits for them, and re-layouts: 10.7 us -> 3.01 us
    pallas_call x5, Pallas kernels: 6.97 us -> 14.4 us  [call(): pl.pallas_call(kernel, out_shape=outs, name=name, in_specs=specs, out_spe...]
    all_to_all x0 -> x1, starting transfers between devices: none -> 5.21 us  [on_device(): lax.all_to_all(found.reshape(blocks, per_peer, width), 'blk', split_axis=...]
    all_to_all x1, starting transfers between devices: 4.54 us -> 7.5 us  [on_device(): got = lax.all_to_all(send, 'blk', split_axis=0, concat_axis=0, tiled=True)]
    ppermute x4, starting transfers between devices: 4.93 us -> 2.11 us  [shifted(): return lax.ppermute(value, axis, pairs)]
  transfers between devices with their start and end apart: 7 -> 8, of which waited for: 3 -> 4; matrix products, arithmetic and copies ran while one was open for 0% -> 0% of each run, Pallas kernels for 5% -> 19%
where the time goes in v2:
time: 59.4 us; the launch traced here: 58.9 us
  starting transfers between devices  19.8 us (33%)
  waiting for transfers between devices  19.7 us (33%)
  Pallas kernels  14.4 us (24%)
  local copies, waits for them, and re-layouts  3.01 us (5%)
  other arithmetic  1.15 us (2%)
  between operations  0.8 us (1%)
    pallas_call x5, Pallas kernels, call(): pl.pallas_call(kernel, out_shape=outs, name=name, in_specs=specs, out_spe...  14.4 us
    all_to_all x1, waiting for transfers between devices, on_device(): got = lax.all_to_all(send, 'blk', split_axis=0, concat_axis=0, tiled=True)  13.4 us
    all_to_all x1, starting transfers between devices, on_device(): got = lax.all_to_all(send, 'blk', split_axis=0, concat_axis=0, tiled=True)  7.5 us
    all_to_all x1, starting transfers between devices, on_device(): lax.all_to_all(found.reshape(blocks, per_peer, width), 'blk', split_axis=...  5.21 us
    ppermute x1, waiting for transfers between devices, on_device(): other_even = lax.ppermute(previous, ('blk', 'mp'), across)  3.5 us
    ppermute x1, starting transfers between devices, on_device(): other_even = lax.ppermute(previous, ('blk', 'mp'), across)  3.43 us
    unnamed x18, local copies, waits for them, and re-layouts  3.01 us
    ppermute x4, waiting for transfers between devices, shifted(): return lax.ppermute(value, axis, pairs)  2.8 us
  transfers between devices with their start and end apart: 8, of which 4 were waited for; matrix products, arithmetic and copies ran while one was open for 0% of the time, Pallas kernels for 19%

profile of v2, /device:TPU:0, one launch (start us, length us, event | category | flops | bytes accessed | tf_op | source)
XLA Modules:
  0.0 58.9 jit_solution(1976831075134448047)
XLA Ops:
  0.6 3.0 %rank.1 = (bf16[16,144,128]{2,1,0:T(8,128)(2,1)}, s32[1,512]{1,0:T(1,128)}) custom-call(s32[512]{0:T(512)} %dev_hbm.1, s32[512]{0:T(512)} %row_hbm.1, bf16[512,512]{1,0:T(8,128)(2,1)} %anchors_ref.3), custom_call_target="tpu_custom_call" | custom-call | flops 67108864 | bytes 1120256 | tf_op jit(solution)/shard_map/rank/pallas_call | solution.py:195
  3.6 0.0 copy-start.2
  3.7 0.0 copy-start.3
  3.7 7.5 %all-to-all-start = ((bf16[16,144,128]{2,1,0:T(8,128)(2,1)}), bf16[16,144,128]{2,1,0:T(8,128)(2,1)S(1)}, u32[]{:S(2)}, u32[]{:S(2)}) async-start(bf16[16,144,128]{2,1,0:T(8,128)(2,1)} %get-tuple-element.12), calls=%async_computation | async-start | bytes 1179648 | tf_op jit(solution)/shard_map/all_to_all | solution.py:230
  11.2 0.0 copy-done.2
  11.2 0.0 copy-start.6
  11.2 1.6 %collective-permute-start = (bf16[512,512]{1,0:T(8,128)(2,1)S(1)}, bf16[512,512]{1,0:T(8,128)(2,1)S(1)}, u32[]{:S(2)}, u32[]{:S(2)}) collective-permute-start(bf16[512,512]{1,0:T(8,128)(2,1)S(1)} %copy-done.2), channel_id=1, source_target_pairs={{0,1},{1,0},{2,3},{3,2},{4,5},{5,4},{6,7},{7,6},{8,9},{9,8},{10,11... | collective-permute-start | bytes 1572872 | tf_op jit(solution)/shard_map/ppermute | solution.py:23
  12.8 0.0 copy-done.3
  12.8 0.5 collective-permute-start.3
  13.3 13.4 %all-to-all-done.got_hbm = bf16[16,144,128]{2,1,0:T(8,128)(2,1)S(1)} async-done(((bf16[16,144,128]{2,1,0:T(8,128)(2,1)}), bf16[16,144,128]{2,1,0:T(8,128)(2,1)S(1)}, u32[]{:S(2)}, u32[]{:S(2)}) %all-to-all-start) | async-done | bytes 589856 | tf_op jit(solution)/shard_map/all_to_all | solution.py:230
  26.7 0.0 copy-start
  26.7 0.0 collective-permute-start.1
  26.7 0.0 collective-permute-done.other_anchors_ref
  26.7 0.8 %copy-done = bf16[16,144,128]{2,1,0:T(8,128)(2,1)} copy-done((bf16[16,144,128]{2,1,0:T(8,128)(2,1)}, bf16[16,144,128]{2,1,0:T(8,128)(2,1)S(1)}, u32[]{:S(2)}) %copy-start) | copy-done | bytes 589848
  27.5 2.4 %serve.1 = bf16[512,512]{1,0:T(8,128)(2,1)} custom-call(bf16[16,144,128]{2,1,0:T(8,128)(2,1)} %copy-done, bf16[512,512]{1,0:T(8,128)(2,1)} %partners_ref.1), custom_call_target="tpu_custom_call" | custom-call | bytes 1638400 | tf_op jit(solution)/shard_map/serve/pallas_call | solution.py:195
  30.0 0.0 copy-start.4
  30.0 0.0 copy-start.8
  30.0 5.2 %all-to-all-start.1 = ((bf16[16,32,512]{2,1,0:T(8,128)(2,1)}), bf16[16,32,512]{2,1,0:T(8,128)(2,1)}, u32[]{:S(2)}, u32[]{:S(2)}) async-start(bf16[16,32,512]{2,1,0:T(8,128)(2,1)} %bitcast.5), calls=%async_computation.1 | async-start | bytes 1048576 | tf_op jit(solution)/shard_map/all_to_all | solution.py:247
  35.2 1.7 %collective-permute-done.3.other_partners_ref = bf16[512,512]{1,0:T(8,128)(2,1)} collective-permute-done((bf16[512,512]{1,0:T(8,128)(2,1)S(1)}, bf16[512,512]{1,0:T(8,128)(2,1)}, u32[]{:S(2)}, u32[]{:S(2)}) %collective-permute-start.3) | collective-permute-done | bytes 524320 | tf_op jit(solution)/shard_map/ppermute | solution.py:23
  36.9 1.6 %collective-permute-start.4 = (bf16[512,512]{1,0:T(8,128)(2,1)}, bf16[512,512]{1,0:T(8,128)(2,1)S(1)}, u32[]{:S(2)}, u32[]{:S(2)}) collective-permute-start(bf16[512,512]{1,0:T(8,128)(2,1)} %collective-permute-done.3.other_partners_ref), channel_id=1, source_target_pairs={{0,2},{4,6},{8,10},{12,14},{16,18},{20,22},{24,26},{28,30},{1,3},{... | collective-permute-start | bytes 1572872 | tf_op jit(solution)/shard_map/ppermute | solution.py:239
  38.4 0.0 collective-permute-done.1.previous_ref
  38.4 3.4 %collective-permute-start.2 = (bf16[512,512]{1,0:T(8,128)(2,1)}, bf16[512,512]{1,0:T(8,128)(2,1)S(1)}, u32[]{:S(2)}, u32[]{:S(2)}) collective-permute-start(bf16[512,512]{1,0:T(8,128)(2,1)} %collective-permute-done.1.previous_ref), channel_id=1, source_target_pairs={{0,1},{1,0},{4,5},{5,4},{8,9},{9,8},{12,13},{13,12},{16,17},{17,16... | collective-permute-start | bytes 1572872 | tf_op jit(solution)/shard_map/ppermute | solution.py:238
  41.9 0.0 copy-done.6
  41.9 0.0 copy-done.4
  41.9 0.0 copy-done.8
  41.9 0.0 copy-start.7
  41.9 1.2 %copy-done.7 = f32[512,512]{1,0:T(8,128)S(1)} copy-done((f32[512,512]{1,0:T(8,128)S(1)}, f32[512,512]{1,0:T(8,128)}, u32[]{:S(2)}) %copy-start.7) | copy-done | bytes 1048600
  43.1 0.0 copy-start.1
  43.1 3.1 %own.1 = (f32[512,512]{1,0:T(8,128)S(1)}, bf16[512,512]{1,0:T(8,128)(2,1)}) custom-call(bf16[512,512]{1,0:T(8,128)(2,1)S(1)} %copy-done.2, bf16[512,512]{1,0:T(8,128)(2,1)S(1)} %collective-permute-done.other_anchors_ref, bf16[512,512]{1,0:T(8,128)(2,1)S(1)} %copy-done.4, bf16[512,512]{1,0:T(8,128)(2,1)} %collective-permute-done.3.other_partners_ref, ...), custom_call_target="tpu_custom_call" | custom-call | flops 1073741824 | bytes 5769216 | tf_op jit(solution)/shard_map/own/pallas_call | solution.py:195
  46.2 0.0 collective-permute-start.5
  46.2 0.0 collective-permute-done.4.other_odd_ref
  46.2 3.5 %collective-permute-done.2.other_even_ref = bf16[512,512]{1,0:T(8,128)(2,1)S(1)} collective-permute-done((bf16[512,512]{1,0:T(8,128)(2,1)}, bf16[512,512]{1,0:T(8,128)(2,1)S(1)}, u32[]{:S(2)}, u32[]{:S(2)}) %collective-permute-start.2) | collective-permute-done | bytes 524320 | tf_op jit(solution)/shard_map/ppermute | solution.py:238
  49.7 0.0 copy-done.1
  49.7 3.0 %prior.1 = (f32[512,512]{1,0:T(8,128)S(1)}, f32[512,512]{1,0:T(8,128)S(1)}) custom-call(bf16[512,512]{1,0:T(8,128)(2,1)S(1)} %copy-done.2, bf16[512,512]{1,0:T(8,128)(2,1)S(1)} %collective-permute-done.other_anchors_ref, bf16[512,512]{1,0:T(8,128)(2,1)} %collective-permute-done.1.previous_ref, bf16[512,512]{1,0:T(8,128)(2,1)S(1)} %collective-permute-done.2.other_even_ref, ...), custom_call_target="tpu_custom_call" | custom-call | flops 1073741824 | bytes 6359040 | tf_op jit(solution)/shard_map/prior/pallas_call | solution.py:195
  52.8 0.0 copy-start.5
  52.8 1.0 %copy-done.5 = f32[512,512]{1,0:T(8,128)} copy-done((f32[512,512]{1,0:T(8,128)}, f32[512,512]{1,0:T(8,128)S(1)}, u32[]{:S(2)}) %copy-start.5) | copy-done | bytes 1048600
  53.8 0.0 all-to-all-done.1
  53.8 2.8 %final.1 = f32[512,512]{1,0:T(8,128)} custom-call(bf16[512,512]{1,0:T(8,128)(2,1)} %bitcast.1.fetched_hbm, s32[1,512]{1,0:T(1,128)} %get-tuple-element.15.slot_hbm, f32[512,512]{1,0:T(8,128)} %copy-done.5), custom_call_target="tpu_custom_call" | custom-call | flops 536870912 | bytes 2623488 | tf_op jit(solution)/shard_map/final/pallas_call | solution.py:195
  56.6 1.1 %collective-permute-done.5 = bf16[512,512]{1,0:T(8,128)(2,1)S(1)} collective-permute-done((bf16[512,512]{1,0:T(8,128)(2,1)}, bf16[512,512]{1,0:T(8,128)(2,1)S(1)}, u32[]{:S(2)}, u32[]{:S(2)}) %collective-permute-start.5) | collective-permute-done | bytes 524320 | tf_op jit(solution)/shard_map/ppermute | solution.py:23
  57.7 1.2 %convert_add_fusion = f32[512,512]{1,0:T(8,128)} fusion(f32[512,512]{1,0:T(8,128)S(1)} %get-tuple-element.21, bf16[512,512]{1,0:T(8,128)(2,1)S(1)} %collective-permute-done.5), kind=kLoop, calls=%fused_computation | loop fusion | flops 524288 | bytes 2621440 | tf_op jit(solution)/shard_map/add | solution.py:267
Async XLA Ops:
  3.6 7.5 %copy-start.2 = (bf16[512,512]{1,0:T(8,128)(2,1)S(1)}, bf16[512,512]{1,0:T(8,128)(2,1)}, u32[]{:S(2)}) copy-start(bf16[512,512]{1,0:T(8,128)(2,1)} %anchors_ref.3) | copy-start | bytes 1572868
  3.7 9.1 %copy-start.3 = (bf16[512,512]{1,0:T(8,128)(2,1)S(1)}, bf16[512,512]{1,0:T(8,128)(2,1)}, u32[]{:S(2)}) copy-start(bf16[512,512]{1,0:T(8,128)(2,1)} %partners_ref.1) | copy-start | bytes 1572868
  3.7 23.1 %all-to-all-start = ((bf16[16,144,128]{2,1,0:T(8,128)(2,1)}), bf16[16,144,128]{2,1,0:T(8,128)(2,1)S(1)}, u32[]{:S(2)}, u32[]{:S(2)}) async-start(bf16[16,144,128]{2,1,0:T(8,128)(2,1)} %get-tuple-element.12), calls=%async_computation | async-start | bytes 1179648 | tf_op jit(solution)/shard_map/all_to_all | solution.py:230
  11.2 30.7 %copy-start.6 = (f32[512,512]{1,0:T(8,128)S(1)}, f32[512,512]{1,0:T(8,128)}, u32[]{:S(2)}) copy-start(f32[512,512]{1,0:T(8,128)} %anchor_acc_ref.1) | copy-start | bytes 3145732
  11.2 15.5 %collective-permute-start = (bf16[512,512]{1,0:T(8,128)(2,1)S(1)}, bf16[512,512]{1,0:T(8,128)(2,1)S(1)}, u32[]{:S(2)}, u32[]{:S(2)}) collective-permute-start(bf16[512,512]{1,0:T(8,128)(2,1)S(1)} %copy-done.2), channel_id=1, source_target_pairs={{0,1},{1,0},{2,3},{3,2},{4,5},{5,4},{6,7},{7,6},{8,9},{9,8},{10,11... | collective-permute-start | bytes 1572872 | tf_op jit(solution)/shard_map/ppermute | solution.py:23
  12.8 24.1 %collective-permute-start.3 = (bf16[512,512]{1,0:T(8,128)(2,1)S(1)}, bf16[512,512]{1,0:T(8,128)(2,1)}, u32[]{:S(2)}, u32[]{:S(2)}) collective-permute-start(bf16[512,512]{1,0:T(8,128)(2,1)S(1)} %copy-done.3), channel_id=1, source_target_pairs={{0,1},{1,0},{2,3},{3,2},{4,5},{5,4},{6,7},{7,6},{8,9},{9,8},{10,11... | collective-permute-start | bytes 1572872 | tf_op jit(solution)/shard_map/ppermute | solution.py:23
  26.7 0.8 %copy-start = (bf16[16,144,128]{2,1,0:T(8,128)(2,1)}, bf16[16,144,128]{2,1,0:T(8,128)(2,1)S(1)}, u32[]{:S(2)}) copy-start(bf16[16,144,128]{2,1,0:T(8,128)(2,1)S(1)} %all-to-all-done.got_hbm) | copy-start | bytes 1769476
  26.7 11.7 %collective-permute-start.1 = (bf16[512,512]{1,0:T(8,128)(2,1)S(1)}, bf16[512,512]{1,0:T(8,128)(2,1)}, u32[]{:S(2)}, u32[]{:S(2)}) collective-permute-start(bf16[512,512]{1,0:T(8,128)(2,1)S(1)} %copy-done.3), channel_id=1, source_target_pairs={{0,2},{2,4},{4,6},{6,8},{8,10},{10,12},{12,14},{14,16},{16,18},{18... | collective-permute-start | bytes 1572872 | tf_op jit(solution)/shard_map/ppermute | solution.py:23
  30.0 11.9 %copy-start.4 = (bf16[512,512]{1,0:T(8,128)(2,1)S(1)}, bf16[512,512]{1,0:T(8,128)(2,1)}, u32[]{:S(2)}) copy-start(bf16[512,512]{1,0:T(8,128)(2,1)} %partners_ref.1) | copy-start | bytes 1572868
  30.0 11.9 %copy-start.8 = (f32[512]{0:T(512)S(1)}, f32[512]{0:T(512)}, u32[]{:S(2)}) copy-start(f32[512]{0:T(512)} %param.9) | copy-start | bytes 6148
  30.0 23.8 %all-to-all-start.1 = ((bf16[16,32,512]{2,1,0:T(8,128)(2,1)}), bf16[16,32,512]{2,1,0:T(8,128)(2,1)}, u32[]{:S(2)}, u32[]{:S(2)}) async-start(bf16[16,32,512]{2,1,0:T(8,128)(2,1)} %bitcast.5), calls=%async_computation.1 | async-start | bytes 1048576 | tf_op jit(solution)/shard_map/all_to_all | solution.py:247
  36.9 9.4 %collective-permute-start.4 = (bf16[512,512]{1,0:T(8,128)(2,1)}, bf16[512,512]{1,0:T(8,128)(2,1)S(1)}, u32[]{:S(2)}, u32[]{:S(2)}) collective-permute-start(bf16[512,512]{1,0:T(8,128)(2,1)} %collective-permute-done.3.other_partners_ref), channel_id=1, source_target_pairs={{0,2},{4,6},{8,10},{12,14},{16,18},{20,22},{24,26},{28,30},{1,3},{... | collective-permute-start | bytes 1572872 | tf_op jit(solution)/shard_map/ppermute | solution.py:239
  38.4 11.3 %collective-permute-start.2 = (bf16[512,512]{1,0:T(8,128)(2,1)}, bf16[512,512]{1,0:T(8,128)(2,1)S(1)}, u32[]{:S(2)}, u32[]{:S(2)}) collective-permute-start(bf16[512,512]{1,0:T(8,128)(2,1)} %collective-permute-done.1.previous_ref), channel_id=1, source_target_pairs={{0,1},{1,0},{4,5},{5,4},{8,9},{9,8},{12,13},{13,12},{16,17},{17,16... | collective-permute-start | bytes 1572872 | tf_op jit(solution)/shard_map/ppermute | solution.py:238
  41.9 1.2 %copy-start.7 = (f32[512,512]{1,0:T(8,128)S(1)}, f32[512,512]{1,0:T(8,128)}, u32[]{:S(2)}) copy-start(f32[512,512]{1,0:T(8,128)} %partner_acc_ref.1) | copy-start | bytes 3145732
  43.1 6.6 %copy-start.1 = (bf16[16,144,128]{2,1,0:T(8,128)(2,1)S(1)}, bf16[16,144,128]{2,1,0:T(8,128)(2,1)}, u32[]{:S(2)}) copy-start(bf16[16,144,128]{2,1,0:T(8,128)(2,1)} %copy-done) | copy-start | bytes 1769476
  46.2 11.5 %collective-permute-start.5 = (bf16[512,512]{1,0:T(8,128)(2,1)}, bf16[512,512]{1,0:T(8,128)(2,1)S(1)}, u32[]{:S(2)}, u32[]{:S(2)}) collective-permute-start(bf16[512,512]{1,0:T(8,128)(2,1)} %get-tuple-element.20), channel_id=1, source_target_pairs={{0,2},{2,4},{4,6},{6,8},{8,10},{10,12},{12,14},{14,16},{16,18},{18... | collective-permute-start | bytes 1572872 | tf_op jit(solution)/shard_map/ppermute | solution.py:23
  52.8 1.0 %copy-start.5 = (f32[512,512]{1,0:T(8,128)}, f32[512,512]{1,0:T(8,128)S(1)}, u32[]{:S(2)}) copy-start(f32[512,512]{1,0:T(8,128)S(1)} %get-tuple-element.19.anchor_hbm) | copy-start | bytes 3145732

commit v3 on v2

--- a/solution.py
+++ b/solution.py
@@ -8,7 +8,7 @@
 
 SCALE = 10.0
 LANES = 128
-EXTRA = 16
+EXTRA = 8
 COST = dict(rank=1, serve=0, own=16, prior=16, final=8)
 MID = 40_000_000
 SERVE = 63_400_000

time: 59.4 us -> 59.4 us (level)
  no operation moved by 1% of the time
where the time goes in v3:
time: 59.4 us; the launch traced here: 58.9 us
  starting transfers between devices  19.9 us (34%)
  waiting for transfers between devices  19.8 us (33%)
  Pallas kernels  14.3 us (24%)
  local copies, waits for them, and re-layouts  3 us (5%)
  other arithmetic  1.15 us (2%)
  between operations  0.8 us (1%)
    pallas_call x5, Pallas kernels, call(): pl.pallas_call(kernel, out_shape=outs, name=name, in_specs=specs, out_spe...  14.3 us
    all_to_all x1, waiting for transfers between devices, on_device(): got = lax.all_to_all(send, 'blk', split_axis=0, concat_axis=0, tiled=True)  12.9 us
    all_to_all x1, starting transfers between devices, on_device(): got = lax.all_to_all(send, 'blk', split_axis=0, concat_axis=0, tiled=True)  7.5 us
    all_to_all x1, starting transfers between devices, on_device(): lax.all_to_all(found.reshape(blocks, per_peer, width), 'blk', split_axis=...  5.26 us
    ppermute x1, waiting for transfers between devices, on_device(): other_even = lax.ppermute(previous, ('blk', 'mp'), across)  3.5 us
    ppermute x1, starting transfers between devices, on_device(): other_even = lax.ppermute(previous, ('blk', 'mp'), across)  3.43 us
    ppermute x4, waiting for transfers between devices, shifted(): return lax.ppermute(value, axis, pairs)  3.37 us
    unnamed x18, local copies, waits for them, and re-layouts  3 us
  transfers between devices with their start and end apart: 8, of which 4 were waited for; matrix products, arithmetic and copies ran while one was open for 0% of the time, Pallas kernels for 19%

profile of v3, /device:TPU:0, one launch (start us, length us, event | category | flops | bytes accessed | tf_op | source)
XLA Modules:
  0.0 58.9 jit_solution(3810882876966121901)
XLA Ops:
  0.6 3.0 %rank.1 = (bf16[16,136,128]{2,1,0:T(8,128)(2,1)}, s32[1,512]{1,0:T(1,128)}) custom-call(s32[512]{0:T(512)} %dev_hbm.1, s32[512]{0:T(512)} %row_hbm.1, bf16[512,512]{1,0:T(8,128)(2,1)} %anchors_ref.3), custom_call_target="tpu_custom_call" | custom-call | flops 67108864 | bytes 1087488 | tf_op jit(solution)/shard_map/rank/pallas_call | solution.py:195
  3.6 0.0 copy-start.2
  3.6 0.0 copy-start.3
  3.6 7.5 %all-to-all-start = ((bf16[16,136,128]{2,1,0:T(8,128)(2,1)}), bf16[16,136,128]{2,1,0:T(8,128)(2,1)S(1)}, u32[]{:S(2)}, u32[]{:S(2)}) async-start(bf16[16,136,128]{2,1,0:T(8,128)(2,1)} %get-tuple-element.12), calls=%async_computation | async-start | bytes 1114112 | tf_op jit(solution)/shard_map/all_to_all | solution.py:230
  11.2 0.0 copy-done.2
  11.2 0.0 copy-start.6
  11.2 1.6 %collective-permute-start = (bf16[512,512]{1,0:T(8,128)(2,1)S(1)}, bf16[512,512]{1,0:T(8,128)(2,1)S(1)}, u32[]{:S(2)}, u32[]{:S(2)}) collective-permute-start(bf16[512,512]{1,0:T(8,128)(2,1)S(1)} %copy-done.2), channel_id=1, source_target_pairs={{0,1},{1,0},{2,3},{3,2},{4,5},{5,4},{6,7},{7,6},{8,9},{9,8},{10,11... | collective-permute-start | bytes 1572872 | tf_op jit(solution)/shard_map/ppermute | solution.py:23
  12.8 0.0 copy-done.3
  12.8 0.5 collective-permute-start.3
  13.3 12.9 %all-to-all-done.got_hbm = bf16[16,136,128]{2,1,0:T(8,128)(2,1)S(1)} async-done(((bf16[16,136,128]{2,1,0:T(8,128)(2,1)}), bf16[16,136,128]{2,1,0:T(8,128)(2,1)S(1)}, u32[]{:S(2)}, u32[]{:S(2)}) %all-to-all-start) | async-done | bytes 557088 | tf_op jit(solution)/shard_map/all_to_all | solution.py:230
  26.2 0.0 copy-start
  26.2 0.0 collective-permute-start.1
  26.2 0.0 collective-permute-done.other_anchors_ref
  26.2 0.8 %copy-done = bf16[16,136,128]{2,1,0:T(8,128)(2,1)} copy-done((bf16[16,136,128]{2,1,0:T(8,128)(2,1)}, bf16[16,136,128]{2,1,0:T(8,128)(2,1)S(1)}, u32[]{:S(2)}) %copy-start) | copy-done | bytes 557080
  27.0 2.3 %serve.1 = bf16[512,512]{1,0:T(8,128)(2,1)} custom-call(bf16[16,136,128]{2,1,0:T(8,128)(2,1)} %copy-done, bf16[512,512]{1,0:T(8,128)(2,1)} %partners_ref.1), custom_call_target="tpu_custom_call" | custom-call | bytes 1605632 | tf_op jit(solution)/shard_map/serve/pallas_call | solution.py:195
  29.3 0.0 copy-start.4
  29.3 0.0 copy-start.8
  29.3 5.3 %all-to-all-start.1 = ((bf16[16,32,512]{2,1,0:T(8,128)(2,1)}), bf16[16,32,512]{2,1,0:T(8,128)(2,1)}, u32[]{:S(2)}, u32[]{:S(2)}) async-start(bf16[16,32,512]{2,1,0:T(8,128)(2,1)} %bitcast.5), calls=%async_computation.1 | async-start | bytes 1048576 | tf_op jit(solution)/shard_map/all_to_all | solution.py:247
  34.6 2.2 %collective-permute-done.3.other_partners_ref = bf16[512,512]{1,0:T(8,128)(2,1)} collective-permute-done((bf16[512,512]{1,0:T(8,128)(2,1)S(1)}, bf16[512,512]{1,0:T(8,128)(2,1)}, u32[]{:S(2)}, u32[]{:S(2)}) %collective-permute-start.3) | collective-permute-done | bytes 524320 | tf_op jit(solution)/shard_map/ppermute | solution.py:23
  36.8 1.6 %collective-permute-start.4 = (bf16[512,512]{1,0:T(8,128)(2,1)}, bf16[512,512]{1,0:T(8,128)(2,1)S(1)}, u32[]{:S(2)}, u32[]{:S(2)}) collective-permute-start(bf16[512,512]{1,0:T(8,128)(2,1)} %collective-permute-done.3.other_partners_ref), channel_id=1, source_target_pairs={{0,2},{4,6},{8,10},{12,14},{16,18},{20,22},{24,26},{28,30},{1,3},{... | collective-permute-start | bytes 1572872 | tf_op jit(solution)/shard_map/ppermute | solution.py:239
  38.4 0.0 collective-permute-done.1.previous_ref
  38.4 3.4 %collective-permute-start.2 = (bf16[512,512]{1,0:T(8,128)(2,1)}, bf16[512,512]{1,0:T(8,128)(2,1)S(1)}, u32[]{:S(2)}, u32[]{:S(2)}) collective-permute-start(bf16[512,512]{1,0:T(8,128)(2,1)} %collective-permute-done.1.previous_ref), channel_id=1, source_target_pairs={{0,1},{1,0},{4,5},{5,4},{8,9},{9,8},{12,13},{13,12},{16,17},{17,16... | collective-permute-start | bytes 1572872 | tf_op jit(solution)/shard_map/ppermute | solution.py:238
  41.9 0.0 copy-done.6
  41.9 0.0 copy-done.4
  41.9 0.0 copy-done.8
  41.9 0.0 copy-start.7
  41.9 1.2 %copy-done.7 = f32[512,512]{1,0:T(8,128)S(1)} copy-done((f32[512,512]{1,0:T(8,128)S(1)}, f32[512,512]{1,0:T(8,128)}, u32[]{:S(2)}) %copy-start.7) | copy-done | bytes 1048600
  43.1 0.0 copy-start.1
  43.1 3.1 %own.1 = (f32[512,512]{1,0:T(8,128)S(1)}, bf16[512,512]{1,0:T(8,128)(2,1)}) custom-call(bf16[512,512]{1,0:T(8,128)(2,1)S(1)} %copy-done.2, bf16[512,512]{1,0:T(8,128)(2,1)S(1)} %collective-permute-done.other_anchors_ref, bf16[512,512]{1,0:T(8,128)(2,1)S(1)} %copy-done.4, bf16[512,512]{1,0:T(8,128)(2,1)} %collective-permute-done.3.other_partners_ref, ...), custom_call_target="tpu_custom_call" | custom-call | flops 1073741824 | bytes 5769216 | tf_op jit(solution)/shard_map/own/pallas_call | solution.py:195
  46.2 0.0 collective-permute-start.5
  46.2 0.0 collective-permute-done.4.other_odd_ref
  46.2 3.5 %collective-permute-done.2.other_even_ref = bf16[512,512]{1,0:T(8,128)(2,1)S(1)} collective-permute-done((bf16[512,512]{1,0:T(8,128)(2,1)}, bf16[512,512]{1,0:T(8,128)(2,1)S(1)}, u32[]{:S(2)}, u32[]{:S(2)}) %collective-permute-start.2) | collective-permute-done | bytes 524320 | tf_op jit(solution)/shard_map/ppermute | solution.py:238
  49.7 0.0 copy-done.1
  49.7 3.1 %prior.1 = (f32[512,512]{1,0:T(8,128)S(1)}, f32[512,512]{1,0:T(8,128)S(1)}) custom-call(bf16[512,512]{1,0:T(8,128)(2,1)S(1)} %copy-done.2, bf16[512,512]{1,0:T(8,128)(2,1)S(1)} %collective-permute-done.other_anchors_ref, bf16[512,512]{1,0:T(8,128)(2,1)} %collective-permute-done.1.previous_ref, bf16[512,512]{1,0:T(8,128)(2,1)S(1)} %collective-permute-done.2.other_even_ref, ...), custom_call_target="tpu_custom_call" | custom-call | flops 1073741824 | bytes 6326272 | tf_op jit(solution)/shard_map/prior/pallas_call | solution.py:195
  52.8 0.0 copy-start.5
  52.8 1.0 %copy-done.5 = f32[512,512]{1,0:T(8,128)} copy-done((f32[512,512]{1,0:T(8,128)}, f32[512,512]{1,0:T(8,128)S(1)}, u32[]{:S(2)}) %copy-start.5) | copy-done | bytes 1048600
  53.7 0.0 all-to-all-done.1
  53.7 2.8 %final.1 = f32[512,512]{1,0:T(8,128)} custom-call(bf16[512,512]{1,0:T(8,128)(2,1)} %bitcast.1.fetched_hbm, s32[1,512]{1,0:T(1,128)} %get-tuple-element.15.slot_hbm, f32[512,512]{1,0:T(8,128)} %copy-done.5), custom_call_target="tpu_custom_call" | custom-call | flops 536870912 | bytes 2623488 | tf_op jit(solution)/shard_map/final/pallas_call | solution.py:195
  56.6 1.1 %collective-permute-done.5 = bf16[512,512]{1,0:T(8,128)(2,1)S(1)} collective-permute-done((bf16[512,512]{1,0:T(8,128)(2,1)}, bf16[512,512]{1,0:T(8,128)(2,1)S(1)}, u32[]{:S(2)}, u32[]{:S(2)}) %collective-permute-start.5) | collective-permute-done | bytes 524320 | tf_op jit(solution)/shard_map/ppermute | solution.py:23
  57.7 1.2 %convert_add_fusion = f32[512,512]{1,0:T(8,128)} fusion(f32[512,512]{1,0:T(8,128)S(1)} %get-tuple-element.21, bf16[512,512]{1,0:T(8,128)(2,1)S(1)} %collective-permute-done.5), kind=kLoop, calls=%fused_computation | loop fusion | flops 524288 | bytes 2621440 | tf_op jit(solution)/shard_map/add | solution.py:267
Async XLA Ops:
  3.6 7.5 %copy-start.2 = (bf16[512,512]{1,0:T(8,128)(2,1)S(1)}, bf16[512,512]{1,0:T(8,128)(2,1)}, u32[]{:S(2)}) copy-start(bf16[512,512]{1,0:T(8,128)(2,1)} %anchors_ref.3) | copy-start | bytes 1572868
  3.6 9.1 %copy-start.3 = (bf16[512,512]{1,0:T(8,128)(2,1)S(1)}, bf16[512,512]{1,0:T(8,128)(2,1)}, u32[]{:S(2)}) copy-start(bf16[512,512]{1,0:T(8,128)(2,1)} %partners_ref.1) | copy-start | bytes 1572868
  3.6 22.5 %all-to-all-start = ((bf16[16,136,128]{2,1,0:T(8,128)(2,1)}), bf16[16,136,128]{2,1,0:T(8,128)(2,1)S(1)}, u32[]{:S(2)}, u32[]{:S(2)}) async-start(bf16[16,136,128]{2,1,0:T(8,128)(2,1)} %get-tuple-element.12), calls=%async_computation | async-start | bytes 1114112 | tf_op jit(solution)/shard_map/all_to_all | solution.py:230
  11.2 30.7 %copy-start.6 = (f32[512,512]{1,0:T(8,128)S(1)}, f32[512,512]{1,0:T(8,128)}, u32[]{:S(2)}) copy-start(f32[512,512]{1,0:T(8,128)} %anchor_acc_ref.1) | copy-start | bytes 3145732
  11.2 15.0 %collective-permute-start = (bf16[512,512]{1,0:T(8,128)(2,1)S(1)}, bf16[512,512]{1,0:T(8,128)(2,1)S(1)}, u32[]{:S(2)}, u32[]{:S(2)}) collective-permute-start(bf16[512,512]{1,0:T(8,128)(2,1)S(1)} %copy-done.2), channel_id=1, source_target_pairs={{0,1},{1,0},{2,3},{3,2},{4,5},{5,4},{6,7},{7,6},{8,9},{9,8},{10,11... | collective-permute-start | bytes 1572872 | tf_op jit(solution)/shard_map/ppermute | solution.py:23
  12.8 24.1 %collective-permute-start.3 = (bf16[512,512]{1,0:T(8,128)(2,1)S(1)}, bf16[512,512]{1,0:T(8,128)(2,1)}, u32[]{:S(2)}, u32[]{:S(2)}) collective-permute-start(bf16[512,512]{1,0:T(8,128)(2,1)S(1)} %copy-done.3), channel_id=1, source_target_pairs={{0,1},{1,0},{2,3},{3,2},{4,5},{5,4},{6,7},{7,6},{8,9},{9,8},{10,11... | collective-permute-start | bytes 1572872 | tf_op jit(solution)/shard_map/ppermute | solution.py:23
  26.2 0.8 %copy-start = (bf16[16,136,128]{2,1,0:T(8,128)(2,1)}, bf16[16,136,128]{2,1,0:T(8,128)(2,1)S(1)}, u32[]{:S(2)}) copy-start(bf16[16,136,128]{2,1,0:T(8,128)(2,1)S(1)} %all-to-all-done.got_hbm) | copy-start | bytes 1671172
  26.2 12.2 %collective-permute-start.1 = (bf16[512,512]{1,0:T(8,128)(2,1)S(1)}, bf16[512,512]{1,0:T(8,128)(2,1)}, u32[]{:S(2)}, u32[]{:S(2)}) collective-permute-start(bf16[512,512]{1,0:T(8,128)(2,1)S(1)} %copy-done.3), channel_id=1, source_target_pairs={{0,2},{2,4},{4,6},{6,8},{8,10},{10,12},{12,14},{14,16},{16,18},{18... | collective-permute-start | bytes 1572872 | tf_op jit(solution)/shard_map/ppermute | solution.py:23
  29.3 12.5 %copy-start.4 = (bf16[512,512]{1,0:T(8,128)(2,1)S(1)}, bf16[512,512]{1,0:T(8,128)(2,1)}, u32[]{:S(2)}) copy-start(bf16[512,512]{1,0:T(8,128)(2,1)} %partners_ref.1) | copy-start | bytes 1572868
  29.3 12.5 %copy-start.8 = (f32[512]{0:T(512)S(1)}, f32[512]{0:T(512)}, u32[]{:S(2)}) copy-start(f32[512]{0:T(512)} %param.9) | copy-start | bytes 6148
  29.3 24.4 %all-to-all-start.1 = ((bf16[16,32,512]{2,1,0:T(8,128)(2,1)}), bf16[16,32,512]{2,1,0:T(8,128)(2,1)}, u32[]{:S(2)}, u32[]{:S(2)}) async-start(bf16[16,32,512]{2,1,0:T(8,128)(2,1)} %bitcast.5), calls=%async_computation.1 | async-start | bytes 1048576 | tf_op jit(solution)/shard_map/all_to_all | solution.py:247
  36.8 9.4 %collective-permute-start.4 = (bf16[512,512]{1,0:T(8,128)(2,1)}, bf16[512,512]{1,0:T(8,128)(2,1)S(1)}, u32[]{:S(2)}, u32[]{:S(2)}) collective-permute-start(bf16[512,512]{1,0:T(8,128)(2,1)} %collective-permute-done.3.other_partners_ref), channel_id=1, source_target_pairs={{0,2},{4,6},{8,10},{12,14},{16,18},{20,22},{24,26},{28,30},{1,3},{... | collective-permute-start | bytes 1572872 | tf_op jit(solution)/shard_map/ppermute | solution.py:239
  38.4 11.3 %collective-permute-start.2 = (bf16[512,512]{1,0:T(8,128)(2,1)}, bf16[512,512]{1,0:T(8,128)(2,1)S(1)}, u32[]{:S(2)}, u32[]{:S(2)}) collective-permute-start(bf16[512,512]{1,0:T(8,128)(2,1)} %collective-permute-done.1.previous_ref), channel_id=1, source_target_pairs={{0,1},{1,0},{4,5},{5,4},{8,9},{9,8},{12,13},{13,12},{16,17},{17,16... | collective-permute-start | bytes 1572872 | tf_op jit(solution)/shard_map/ppermute | solution.py:238
  41.9 1.2 %copy-start.7 = (f32[512,512]{1,0:T(8,128)S(1)}, f32[512,512]{1,0:T(8,128)}, u32[]{:S(2)}) copy-start(f32[512,512]{1,0:T(8,128)} %partner_acc_ref.1) | copy-start | bytes 3145732
  43.1 6.6 %copy-start.1 = (bf16[16,136,128]{2,1,0:T(8,128)(2,1)S(1)}, bf16[16,136,128]{2,1,0:T(8,128)(2,1)}, u32[]{:S(2)}) copy-start(bf16[16,136,128]{2,1,0:T(8,128)(2,1)} %copy-done) | copy-start | bytes 1671172
  46.2 11.5 %collective-permute-start.5 = (bf16[512,512]{1,0:T(8,128)(2,1)}, bf16[512,512]{1,0:T(8,128)(2,1)S(1)}, u32[]{:S(2)}, u32[]{:S(2)}) collective-permute-start(bf16[512,512]{1,0:T(8,128)(2,1)} %get-tuple-element.20), channel_id=1, source_target_pairs={{0,2},{2,4},{4,6},{6,8},{8,10},{10,12},{12,14},{14,16},{16,18},{18... | collective-permute-start | bytes 1572872 | tf_op jit(solution)/shard_map/ppermute | solution.py:23
  52.8 1.0 %copy-start.5 = (f32[512,512]{1,0:T(8,128)}, f32[512,512]{1,0:T(8,128)S(1)}, u32[]{:S(2)}) copy-start(f32[512,512]{1,0:T(8,128)S(1)} %get-tuple-element.19.anchor_hbm) | copy-start | bytes 3145732

commit v4 on v3

--- a/solution.py
+++ b/solution.py
@@ -233,7 +233,6 @@
     other_partners = shifted(partners, "mp", 1)
     got, ring_partners = lax.optimization_barrier((got, partners))
     previous = shifted(ring_partners, "blk", 1)
-    got, other_anchors = lax.optimization_barrier((got, other_anchors))
     across = [(2 * block + half, 2 * block + 1 - half) for block in range(0, blocks, 2) for half in range(2)]
     other_even = lax.ppermute(previous, ("blk", "mp"), across)
     other_odd = lax.ppermute(other_partners, "blk", [(block, block + 1) for block in range(0, blocks, 2)])
@@ -244,6 +243,7 @@
         (got, partners), spaces="hh", limit=SERVE,
         scratch=(pltpu.VMEM((blocks, EXTRA, LANES), BF16), pltpu.VMEM((rows, width), BF16), dma((2,))),
     )
+    found, other_anchors = lax.optimization_barrier((found, other_anchors))
     fetched = lax.all_to_all(
         found.reshape(blocks, per_peer, width), "blk", split_axis=0, concat_axis=0, tiled=True
     ).reshape(rows, width)

time: 59.4 us -> 59.4 us (level)
  no operation moved by 1% of the time
where the time goes in v4:
time: 59.4 us; the launch traced here: 58.9 us
  starting transfers between devices  19.8 us (33%)
  waiting for transfers between devices  19.8 us (33%)
  Pallas kernels  14.3 us (24%)
  local copies, waits for them, and re-layouts  3.01 us (5%)
  other arithmetic  1.15 us (2%)
  between operations  0.81 us (1%)
    pallas_call x5, Pallas kernels, call(): pl.pallas_call(kernel, out_shape=outs, name=name, in_specs=specs, out_spe...  14.3 us
    all_to_all x1, waiting for transfers between devices, on_device(): got = lax.all_to_all(send, 'blk', split_axis=0, concat_axis=0, tiled=True)  12.9 us
    all_to_all x1, starting transfers between devices, on_device(): got = lax.all_to_all(send, 'blk', split_axis=0, concat_axis=0, tiled=True)  7.5 us
    all_to_all x1, starting transfers between devices, on_device(): lax.all_to_all(found.reshape(blocks, per_peer, width), 'blk', split_axis=...  5.22 us
    ppermute x1, waiting for transfers between devices, on_device(): other_even = lax.ppermute(previous, ('blk', 'mp'), across)  3.5 us
    ppermute x1, starting transfers between devices, on_device(): other_even = lax.ppermute(previous, ('blk', 'mp'), across)  3.43 us
    ppermute x4, waiting for transfers between devices, shifted(): return lax.ppermute(value, axis, pairs)  3.4 us
    unnamed x18, local copies, waits for them, and re-layouts  3.01 us
  transfers between devices with their start and end apart: 8, of which 4 were waited for; matrix products, arithmetic and copies ran while one was open for 0% of the time, Pallas kernels for 19%

profile of v4, /device:TPU:0, one launch (start us, length us, event | category | flops | bytes accessed | tf_op | source)
XLA Modules:
  0.0 58.9 jit_solution(10882397800362369480)
XLA Ops:
  0.6 3.0 %rank.1 = (bf16[16,136,128]{2,1,0:T(8,128)(2,1)}, s32[1,512]{1,0:T(1,128)}) custom-call(s32[512]{0:T(512)} %dev_hbm.1, s32[512]{0:T(512)} %row_hbm.1, bf16[512,512]{1,0:T(8,128)(2,1)} %anchors_ref.3), custom_call_target="tpu_custom_call" | custom-call | flops 67108864 | bytes 1087488 | tf_op jit(solution)/shard_map/rank/pallas_call | solution.py:195
  3.6 0.0 copy-start.2
  3.6 0.0 copy-start.3
  3.6 7.5 %all-to-all-start = ((bf16[16,136,128]{2,1,0:T(8,128)(2,1)}), bf16[16,136,128]{2,1,0:T(8,128)(2,1)S(1)}, u32[]{:S(2)}, u32[]{:S(2)}) async-start(bf16[16,136,128]{2,1,0:T(8,128)(2,1)} %get-tuple-element.12), calls=%async_computation | async-start | bytes 1114112 | tf_op jit(solution)/shard_map/all_to_all | solution.py:230
  11.2 0.0 copy-done.2
  11.2 0.0 copy-start.6
  11.2 1.6 %collective-permute-start = (bf16[512,512]{1,0:T(8,128)(2,1)S(1)}, bf16[512,512]{1,0:T(8,128)(2,1)S(1)}, u32[]{:S(2)}, u32[]{:S(2)}) collective-permute-start(bf16[512,512]{1,0:T(8,128)(2,1)S(1)} %copy-done.2), channel_id=1, source_target_pairs={{0,1},{1,0},{2,3},{3,2},{4,5},{5,4},{6,7},{7,6},{8,9},{9,8},{10,11... | collective-permute-start | bytes 1572872 | tf_op jit(solution)/shard_map/ppermute | solution.py:23
  12.8 0.0 copy-done.3
  12.8 0.5 collective-permute-start.3
  13.3 12.9 %all-to-all-done.got_hbm = bf16[16,136,128]{2,1,0:T(8,128)(2,1)S(1)} async-done(((bf16[16,136,128]{2,1,0:T(8,128)(2,1)}), bf16[16,136,128]{2,1,0:T(8,128)(2,1)S(1)}, u32[]{:S(2)}, u32[]{:S(2)}) %all-to-all-start) | async-done | bytes 557088 | tf_op jit(solution)/shard_map/all_to_all | solution.py:230
  26.2 0.0 copy-start
  26.2 0.0 collective-permute-start.1
  26.2 0.8 %copy-done = bf16[16,136,128]{2,1,0:T(8,128)(2,1)} copy-done((bf16[16,136,128]{2,1,0:T(8,128)(2,1)}, bf16[16,136,128]{2,1,0:T(8,128)(2,1)S(1)}, u32[]{:S(2)}) %copy-start) | copy-done | bytes 557080
  27.0 2.3 %serve.1 = bf16[512,512]{1,0:T(8,128)(2,1)} custom-call(bf16[16,136,128]{2,1,0:T(8,128)(2,1)} %copy-done, bf16[512,512]{1,0:T(8,128)(2,1)} %partners_ref.1), custom_call_target="tpu_custom_call" | custom-call | bytes 1605632 | tf_op jit(solution)/shard_map/serve/pallas_call | solution.py:195
  29.3 0.0 collective-permute-done.other_anchors_ref
  29.3 0.0 copy-start.4
  29.3 0.0 copy-start.8
  29.4 5.2 %all-to-all-start.1 = ((bf16[16,32,512]{2,1,0:T(8,128)(2,1)}), bf16[16,32,512]{2,1,0:T(8,128)(2,1)}, u32[]{:S(2)}, u32[]{:S(2)}) async-start(bf16[16,32,512]{2,1,0:T(8,128)(2,1)} %bitcast.5), calls=%async_computation.1 | async-start | bytes 1048576 | tf_op jit(solution)/shard_map/all_to_all | solution.py:247
  34.6 2.3 %collective-permute-done.3.other_partners_ref = bf16[512,512]{1,0:T(8,128)(2,1)} collective-permute-done((bf16[512,512]{1,0:T(8,128)(2,1)S(1)}, bf16[512,512]{1,0:T(8,128)(2,1)}, u32[]{:S(2)}, u32[]{:S(2)}) %collective-permute-start.3) | collective-permute-done | bytes 524320 | tf_op jit(solution)/shard_map/ppermute | solution.py:23
  36.8 1.6 %collective-permute-start.4 = (bf16[512,512]{1,0:T(8,128)(2,1)}, bf16[512,512]{1,0:T(8,128)(2,1)S(1)}, u32[]{:S(2)}, u32[]{:S(2)}) collective-permute-start(bf16[512,512]{1,0:T(8,128)(2,1)} %collective-permute-done.3.other_partners_ref), channel_id=1, source_target_pairs={{0,2},{4,6},{8,10},{12,14},{16,18},{20,22},{24,26},{28,30},{1,3},{... | collective-permute-start | bytes 1572872 | tf_op jit(solution)/shard_map/ppermute | solution.py:238
  38.4 0.0 collective-permute-done.1.previous_ref
  38.4 3.4 %collective-permute-start.2 = (bf16[512,512]{1,0:T(8,128)(2,1)}, bf16[512,512]{1,0:T(8,128)(2,1)S(1)}, u32[]{:S(2)}, u32[]{:S(2)}) collective-permute-start(bf16[512,512]{1,0:T(8,128)(2,1)} %collective-permute-done.1.previous_ref), channel_id=1, source_target_pairs={{0,1},{1,0},{4,5},{5,4},{8,9},{9,8},{12,13},{13,12},{16,17},{17,16... | collective-permute-start | bytes 1572872 | tf_op jit(solution)/shard_map/ppermute | solution.py:237
  41.9 0.0 copy-done.6
  41.9 0.0 copy-done.4
  41.9 0.0 copy-done.8
  41.9 0.0 copy-start.7
  41.9 1.2 %copy-done.7 = f32[512,512]{1,0:T(8,128)S(1)} copy-done((f32[512,512]{1,0:T(8,128)S(1)}, f32[512,512]{1,0:T(8,128)}, u32[]{:S(2)}) %copy-start.7) | copy-done | bytes 1048600
  43.1 0.0 copy-start.1
  43.1 3.1 %own.1 = (f32[512,512]{1,0:T(8,128)S(1)}, bf16[512,512]{1,0:T(8,128)(2,1)}) custom-call(bf16[512,512]{1,0:T(8,128)(2,1)S(1)} %copy-done.2, bf16[512,512]{1,0:T(8,128)(2,1)S(1)} %collective-permute-done.other_anchors_ref, bf16[512,512]{1,0:T(8,128)(2,1)S(1)} %copy-done.4, bf16[512,512]{1,0:T(8,128)(2,1)} %collective-permute-done.3.other_partners_ref, ...), custom_call_target="tpu_custom_call" | custom-call | flops 1073741824 | bytes 5769216 | tf_op jit(solution)/shard_map/own/pallas_call | solution.py:195
  46.2 0.0 collective-permute-start.5
  46.2 0.0 collective-permute-done.4.other_odd_ref
  46.2 3.5 %collective-permute-done.2.other_even_ref = bf16[512,512]{1,0:T(8,128)(2,1)S(1)} collective-permute-done((bf16[512,512]{1,0:T(8,128)(2,1)}, bf16[512,512]{1,0:T(8,128)(2,1)S(1)}, u32[]{:S(2)}, u32[]{:S(2)}) %collective-permute-start.2) | collective-permute-done | bytes 524320 | tf_op jit(solution)/shard_map/ppermute | solution.py:237
  49.7 0.0 copy-done.1
  49.7 3.1 %prior.1 = (f32[512,512]{1,0:T(8,128)S(1)}, f32[512,512]{1,0:T(8,128)S(1)}) custom-call(bf16[512,512]{1,0:T(8,128)(2,1)S(1)} %copy-done.2, bf16[512,512]{1,0:T(8,128)(2,1)S(1)} %collective-permute-done.other_anchors_ref, bf16[512,512]{1,0:T(8,128)(2,1)} %collective-permute-done.1.previous_ref, bf16[512,512]{1,0:T(8,128)(2,1)S(1)} %collective-permute-done.2.other_even_ref, ...), custom_call_target="tpu_custom_call" | custom-call | flops 1073741824 | bytes 6326272 | tf_op jit(solution)/shard_map/prior/pallas_call | solution.py:195
  52.8 0.0 copy-start.5
  52.8 1.0 %copy-done.5 = f32[512,512]{1,0:T(8,128)} copy-done((f32[512,512]{1,0:T(8,128)}, f32[512,512]{1,0:T(8,128)S(1)}, u32[]{:S(2)}) %copy-start.5) | copy-done | bytes 1048600
  53.7 0.0 all-to-all-done.1
  53.7 2.8 %final.1 = f32[512,512]{1,0:T(8,128)} custom-call(bf16[512,512]{1,0:T(8,128)(2,1)} %bitcast.1.fetched_hbm, s32[1,512]{1,0:T(1,128)} %get-tuple-element.15.slot_hbm, f32[512,512]{1,0:T(8,128)} %copy-done.5), custom_call_target="tpu_custom_call" | custom-call | flops 536870912 | bytes 2623488 | tf_op jit(solution)/shard_map/final/pallas_call | solution.py:195
  56.6 1.1 %collective-permute-done.5 = bf16[512,512]{1,0:T(8,128)(2,1)S(1)} collective-permute-done((bf16[512,512]{1,0:T(8,128)(2,1)}, bf16[512,512]{1,0:T(8,128)(2,1)S(1)}, u32[]{:S(2)}, u32[]{:S(2)}) %collective-permute-start.5) | collective-permute-done | bytes 524320 | tf_op jit(solution)/shard_map/ppermute | solution.py:23
  57.7 1.2 %convert_add_fusion = f32[512,512]{1,0:T(8,128)} fusion(f32[512,512]{1,0:T(8,128)S(1)} %get-tuple-element.21, bf16[512,512]{1,0:T(8,128)(2,1)S(1)} %collective-permute-done.5), kind=kLoop, calls=%fused_computation | loop fusion | flops 524288 | bytes 2621440 | tf_op jit(solution)/shard_map/add | solution.py:267
Async XLA Ops:
  3.6 7.5 %copy-start.2 = (bf16[512,512]{1,0:T(8,128)(2,1)S(1)}, bf16[512,512]{1,0:T(8,128)(2,1)}, u32[]{:S(2)}) copy-start(bf16[512,512]{1,0:T(8,128)(2,1)} %anchors_ref.3) | copy-start | bytes 1572868
  3.6 9.1 %copy-start.3 = (bf16[512,512]{1,0:T(8,128)(2,1)S(1)}, bf16[512,512]{1,0:T(8,128)(2,1)}, u32[]{:S(2)}) copy-start(bf16[512,512]{1,0:T(8,128)(2,1)} %partners_ref.1) | copy-start | bytes 1572868
  3.6 22.5 %all-to-all-start = ((bf16[16,136,128]{2,1,0:T(8,128)(2,1)}), bf16[16,136,128]{2,1,0:T(8,128)(2,1)S(1)}, u32[]{:S(2)}, u32[]{:S(2)}) async-start(bf16[16,136,128]{2,1,0:T(8,128)(2,1)} %get-tuple-element.12), calls=%async_computation | async-start | bytes 1114112 | tf_op jit(solution)/shard_map/all_to_all | solution.py:230
  11.2 30.7 %copy-start.6 = (f32[512,512]{1,0:T(8,128)S(1)}, f32[512,512]{1,0:T(8,128)}, u32[]{:S(2)}) copy-start(f32[512,512]{1,0:T(8,128)} %anchor_acc_ref.1) | copy-start | bytes 3145732
  11.2 18.1 %collective-permute-start = (bf16[512,512]{1,0:T(8,128)(2,1)S(1)}, bf16[512,512]{1,0:T(8,128)(2,1)S(1)}, u32[]{:S(2)}, u32[]{:S(2)}) collective-permute-start(bf16[512,512]{1,0:T(8,128)(2,1)S(1)} %copy-done.2), channel_id=1, source_target_pairs={{0,1},{1,0},{2,3},{3,2},{4,5},{5,4},{6,7},{7,6},{8,9},{9,8},{10,11... | collective-permute-start | bytes 1572872 | tf_op jit(solution)/shard_map/ppermute | solution.py:23
  12.8 24.1 %collective-permute-start.3 = (bf16[512,512]{1,0:T(8,128)(2,1)S(1)}, bf16[512,512]{1,0:T(8,128)(2,1)}, u32[]{:S(2)}, u32[]{:S(2)}) collective-permute-start(bf16[512,512]{1,0:T(8,128)(2,1)S(1)} %copy-done.3), channel_id=1, source_target_pairs={{0,1},{1,0},{2,3},{3,2},{4,5},{5,4},{6,7},{7,6},{8,9},{9,8},{10,11... | collective-permute-start | bytes 1572872 | tf_op jit(solution)/shard_map/ppermute | solution.py:23
  26.2 0.8 %copy-start = (bf16[16,136,128]{2,1,0:T(8,128)(2,1)}, bf16[16,136,128]{2,1,0:T(8,128)(2,1)S(1)}, u32[]{:S(2)}) copy-start(bf16[16,136,128]{2,1,0:T(8,128)(2,1)S(1)} %all-to-all-done.got_hbm) | copy-start | bytes 1671172
  26.2 12.2 %collective-permute-start.1 = (bf16[512,512]{1,0:T(8,128)(2,1)S(1)}, bf16[512,512]{1,0:T(8,128)(2,1)}, u32[]{:S(2)}, u32[]{:S(2)}) collective-permute-start(bf16[512,512]{1,0:T(8,128)(2,1)S(1)} %copy-done.3), channel_id=1, source_target_pairs={{0,2},{2,4},{4,6},{6,8},{8,10},{10,12},{12,14},{14,16},{16,18},{18... | collective-permute-start | bytes 1572872 | tf_op jit(solution)/shard_map/ppermute | solution.py:23
  29.3 12.5 %copy-start.4 = (bf16[512,512]{1,0:T(8,128)(2,1)S(1)}, bf16[512,512]{1,0:T(8,128)(2,1)}, u32[]{:S(2)}) copy-start(bf16[512,512]{1,0:T(8,128)(2,1)} %partners_ref.1) | copy-start | bytes 1572868
  29.3 12.5 %copy-start.8 = (f32[512]{0:T(512)S(1)}, f32[512]{0:T(512)}, u32[]{:S(2)}) copy-start(f32[512]{0:T(512)} %param.9) | copy-start | bytes 6148
  29.4 24.4 %all-to-all-start.1 = ((bf16[16,32,512]{2,1,0:T(8,128)(2,1)}), bf16[16,32,512]{2,1,0:T(8,128)(2,1)}, u32[]{:S(2)}, u32[]{:S(2)}) async-start(bf16[16,32,512]{2,1,0:T(8,128)(2,1)} %bitcast.5), calls=%async_computation.1 | async-start | bytes 1048576 | tf_op jit(solution)/shard_map/all_to_all | solution.py:247
  36.8 9.4 %collective-permute-start.4 = (bf16[512,512]{1,0:T(8,128)(2,1)}, bf16[512,512]{1,0:T(8,128)(2,1)S(1)}, u32[]{:S(2)}, u32[]{:S(2)}) collective-permute-start(bf16[512,512]{1,0:T(8,128)(2,1)} %collective-permute-done.3.other_partners_ref), channel_id=1, source_target_pairs={{0,2},{4,6},{8,10},{12,14},{16,18},{20,22},{24,26},{28,30},{1,3},{... | collective-permute-start | bytes 1572872 | tf_op jit(solution)/shard_map/ppermute | solution.py:238
  38.4 11.3 %collective-permute-start.2 = (bf16[512,512]{1,0:T(8,128)(2,1)}, bf16[512,512]{1,0:T(8,128)(2,1)S(1)}, u32[]{:S(2)}, u32[]{:S(2)}) collective-permute-start(bf16[512,512]{1,0:T(8,128)(2,1)} %collective-permute-done.1.previous_ref), channel_id=1, source_target_pairs={{0,1},{1,0},{4,5},{5,4},{8,9},{9,8},{12,13},{13,12},{16,17},{17,16... | collective-permute-start | bytes 1572872 | tf_op jit(solution)/shard_map/ppermute | solution.py:237
  41.9 1.2 %copy-start.7 = (f32[512,512]{1,0:T(8,128)S(1)}, f32[512,512]{1,0:T(8,128)}, u32[]{:S(2)}) copy-start(f32[512,512]{1,0:T(8,128)} %partner_acc_ref.1) | copy-start | bytes 3145732
  43.1 6.6 %copy-start.1 = (bf16[16,136,128]{2,1,0:T(8,128)(2,1)S(1)}, bf16[16,136,128]{2,1,0:T(8,128)(2,1)}, u32[]{:S(2)}) copy-start(bf16[16,136,128]{2,1,0:T(8,128)(2,1)} %copy-done) | copy-start | bytes 1671172
  46.2 11.5 %collective-permute-start.5 = (bf16[512,512]{1,0:T(8,128)(2,1)}, bf16[512,512]{1,0:T(8,128)(2,1)S(1)}, u32[]{:S(2)}, u32[]{:S(2)}) collective-permute-start(bf16[512,512]{1,0:T(8,128)(2,1)} %get-tuple-element.20), channel_id=1, source_target_pairs={{0,2},{2,4},{4,6},{6,8},{8,10},{10,12},{12,14},{14,16},{16,18},{18... | collective-permute-start | bytes 1572872 | tf_op jit(solution)/shard_map/ppermute | solution.py:23
  52.8 1.0 %copy-start.5 = (f32[512,512]{1,0:T(8,128)}, f32[512,512]{1,0:T(8,128)S(1)}, u32[]{:S(2)}) copy-start(f32[512,512]{1,0:T(8,128)S(1)} %get-tuple-element.19.anchor_hbm) | copy-start | bytes 3145732
